TPU v7x, 256 devices: a whole 4x4x8 slice. The times are simulated.
256 devices in a mesh: user: 32 (over x_lo, z, core), tensor: 8 (over y, x_hi).
Axes of the slice: x: 4 (x_hi: 2, x_lo: 2; x = x_hi * 2 + x_lo), y: 4, z: 8, core: 2. Of those that a mesh axis runs over, the one named last changes fastest.
Arguments:
- events: bfloat16 [1024, 128, 1024], P('user', None, 'tensor'), may hold values from -6 to 6
- cotangent: bfloat16 [1024, 128, 1024], P('user', None, 'tensor'), may hold values from -6 to 6
- w_in: bfloat16 [1024, 4096], P('user', 'tensor'), may hold values from -0.1875 to 0.1875
- w_out: bfloat16 [1024, 1024], P('user', 'tensor'), may hold values from -0.1875 to 0.1875
- slot_source: int32 [1024], P('user'), may hold values from 0 to 31, as said below
- slot_length: int32 [1024], P('user'), may hold values from 1 to 127, as said below
Outputs:
- grad_x: bfloat16 [1024, 128, 1024], P('user', None, 'tensor')
- grad_w_in: float32 [1024, 4096], P('user', 'tensor')
- grad_w_out: float32 [1024, 1024], P('user', 'tensor')
Inputs may be any that keep to these rules, and one draw needn't show every extreme that they name: `slot_source`: the 32 slots of one host name distinct user shards, and for each slot j the entries h * 32 + j over all hosts h name every user shard once, so every history is placed exactly once. `slot_length`: the 32 slot lengths of one host sum to 2048.
All inputs are finite; a program needn't handle non-finite values.
Results may differ from a plain program's by a relative error of at most 0.023.
Values may be sent and summed in bfloat16 or wider, within the bound.
A program may use at most 128 MiB of HBM per device.

v0:
```python
import math

import jax
import jax.numpy as jnp
from jax import lax
from jax.sharding import PartitionSpec as P

HEAD_DIM = 128
SEQ_LEN = 128


eps = 1e-05


def silu_grad(t):
    sig = jax.nn.sigmoid(t)
    return sig * (1.0 + t * (1.0 - sig))


def host_rows(lengths, sources, total_rows, hist):
    ends = jnp.cumsum(lengths)
    starts = ends - lengths
    rows = jnp.arange(total_rows, dtype=jnp.int32)
    segment = jnp.sum((rows[:, None] >= ends[None, :]).astype(jnp.int32), axis=1)
    onehot = (segment[:, None] == jnp.arange(hist, dtype=jnp.int32)[None, :]).astype(jnp.int32)
    position = rows - jnp.sum(onehot * starts[None, :], axis=1)
    source = jnp.sum(onehot * sources[None, :], axis=1)
    return (segment, position, source, starts)


def local(events, cotangent, w_in, w_out, slot_source, slot_length):
    users = lax.axis_size("user")
    hist, seq_len, width_part = events.shape
    total_rows = hist // 2 * seq_len
    table = lax.all_gather(slot_source, "user", axis=0, tiled=True).reshape(users, hist)
    myself = lax.axis_index("user")
    matches = (table == myself).astype(jnp.int32)
    host_ids = jnp.arange(users, dtype=jnp.int32)[:, None]
    host_of = jnp.sum(matches * host_ids, axis=0)
    send_x = jnp.zeros_like(events).at[host_of].set(events)
    send_d = jnp.zeros_like(cotangent).at[host_of].set(cotangent)
    recv_x, recv_d = (
        lax.all_to_all(send_x, "user", split_axis=0, concat_axis=0, tiled=True),
        lax.all_to_all(send_d, "user", split_axis=0, concat_axis=0, tiled=True),
    )
    segment, position, source, starts = host_rows(slot_length, slot_source, total_rows, hist)
    index = source * seq_len + position
    xp = jnp.take(recv_x.reshape(users * seq_len, width_part), index, axis=0)
    dp = jnp.take(recv_d.reshape(users * seq_len, width_part), index, axis=0)
    x_full, d_full = (
        lax.all_gather(xp, "tensor", axis=1, tiled=True),
        lax.all_gather(dp, "tensor", axis=1, tiled=True),
    )
    w_in_cols = lax.all_gather(w_in, "user", axis=0, tiled=True)
    w_out_cols = lax.all_gather(w_out, "user", axis=0, tiled=True)
    xf = x_full.astype(jnp.float32)
    centred = xf - jnp.mean(xf, axis=1, keepdims=True)
    rstd = lax.rsqrt(jnp.mean(centred * centred, axis=1, keepdims=True) + eps)
    nf = centred * rstd
    nb = nf.astype(jnp.bfloat16)
    z = jnp.dot(nb, w_in_cols, preferred_element_type=jnp.float32)
    local_heads = w_in_cols.shape[1] // (4 * HEAD_DIM)
    g = (
        jax.nn.silu(z)
        .astype(jnp.bfloat16)
        .reshape(total_rows, local_heads, 4, HEAD_DIM)
        .transpose(1, 2, 0, 3)
    )
    upart, vpart, qpart, kpart = (g[:, 0], g[:, 1], g[:, 2], g[:, 3])
    dh = (
        jnp.dot(d_full, w_out_cols, preferred_element_type=jnp.float32)
        .reshape(total_rows, local_heads, HEAD_DIM)
        .transpose(1, 0, 2)
    )
    scale = HEAD_DIM ** (-0.5)
    block = math.gcd(total_rows, 512)
    hparts, grads_u, grads_q = ([], [], [])
    grad_v = jnp.zeros((local_heads, total_rows, HEAD_DIM), jnp.float32)
    grad_k = jnp.zeros((local_heads, total_rows, HEAD_DIM), jnp.float32)
    for number in range(total_rows // block):
        lo = number * block
        hi = lo + block
        mask = (segment[lo:hi, None] == segment[None, :]) & (
            position[None, :] <= position[lo:hi, None]
        )
        q_rows = qpart[:, lo:hi]
        scores = (
            jnp.einsum("hqe,hke->hqk", q_rows, kpart, preferred_element_type=jnp.float32) * scale
        )
        attn = jnp.where(mask[None], jax.nn.silu(scores) / SEQ_LEN, 0.0).astype(jnp.bfloat16)
        yval = jnp.einsum("hqk,hke->hqe", attn, vpart, preferred_element_type=jnp.float32)
        ycen = yval - jnp.mean(yval, axis=2, keepdims=True)
        yrstd = lax.rsqrt(jnp.mean(ycen * ycen, axis=2, keepdims=True) + eps)
        ynorm = ycen * yrstd
        uf = upart[:, lo:hi].astype(jnp.float32)
        hparts.append((ynorm * uf).astype(jnp.bfloat16))
        grad_h = dh[:, lo:hi]
        grads_u.append(grad_h * ynorm)
        grad_yn = grad_h * uf
        grad_y = (
            (
                grad_yn
                - jnp.mean(grad_yn, axis=2, keepdims=True)
                - ynorm * jnp.mean(grad_yn * ynorm, axis=2, keepdims=True)
            )
            * yrstd
        ).astype(jnp.bfloat16)
        grad_a = jnp.einsum("hqe,hke->hqk", grad_y, vpart, preferred_element_type=jnp.float32)
        grad_v = grad_v + jnp.einsum(
            "hqk,hqe->hke", attn, grad_y, preferred_element_type=jnp.float32
        )
        grad_s = jnp.where(mask[None], grad_a * silu_grad(scores) * (scale / SEQ_LEN), 0.0).astype(
            jnp.bfloat16
        )
        grads_q.append(
            jnp.einsum("hqk,hke->hqe", grad_s, kpart, preferred_element_type=jnp.float32)
        )
        grad_k = grad_k + jnp.einsum(
            "hqk,hqe->hke", grad_s, q_rows, preferred_element_type=jnp.float32
        )
    hb = (
        jnp.concatenate(hparts, axis=1)
        .transpose(1, 0, 2)
        .reshape(total_rows, local_heads * HEAD_DIM)
    )
    grad_u = jnp.concatenate(grads_u, axis=1)
    grad_q = jnp.concatenate(grads_q, axis=1)
    dgrad = (
        jnp.stack([grad_u, grad_v, grad_q, grad_k], axis=1)
        .transpose(2, 0, 1, 3)
        .reshape(total_rows, 4 * local_heads * HEAD_DIM)
    )
    dz = (dgrad * silu_grad(z)).astype(jnp.bfloat16)
    columns = d_full
    grad_w_out = lax.psum_scatter(
        lax.dot_general(
            columns, hb, (((0,), (0,)), ((), ())), preferred_element_type=jnp.float32
        ).astype(jnp.bfloat16),
        "user",
        scatter_dimension=0,
        tiled=True,
    ).astype(jnp.float32)
    columns = nb
    grad_w_in = lax.psum_scatter(
        lax.dot_general(
            columns, dz, (((0,), (0,)), ((), ())), preferred_element_type=jnp.float32
        ).astype(jnp.bfloat16),
        "user",
        scatter_dimension=0,
        tiled=True,
    ).astype(jnp.float32)
    dn = lax.dot_general(
        dz, w_in_cols, (((1,), (1,)), ((), ())), preferred_element_type=jnp.float32
    )
    first_col = lax.axis_index("tensor") * width_part
    n_share = lax.dynamic_slice_in_dim(nf, first_col, width_part, 1)
    dn_all = lax.psum(dn, "tensor")
    mean_one = jnp.mean(dn_all, axis=1, keepdims=True)
    mean_two = jnp.mean(dn_all * nf, axis=1, keepdims=True)
    dn_share = lax.dynamic_slice_in_dim(dn_all, first_col, width_part, 1)
    branch = (dn_share - mean_one - n_share * mean_two) * rstd
    dxp = (dp.astype(jnp.float32) + branch).astype(jnp.bfloat16)
    slots = jnp.arange(seq_len, dtype=jnp.int32)
    rows_at = jnp.minimum(starts[:, None] + slots[None, :], total_rows - 1)
    valid = slots[None, :] < slot_length[:, None]
    padded = jnp.take(dxp, rows_at.reshape(-1), axis=0).reshape(hist, seq_len, width_part)
    padded = jnp.where(valid[:, :, None], padded, jnp.zeros_like(padded))
    back = jnp.zeros((users, seq_len, width_part), jnp.bfloat16).at[slot_source].set(padded)
    returned = lax.all_to_all(back, "user", split_axis=0, concat_axis=0, tiled=True)
    grad_x = jnp.take(returned, host_of, axis=0)
    return (grad_x, grad_w_in, grad_w_out)


def solution(mesh):
    in_specs = (
        P("user", None, "tensor"),
        P("user", None, "tensor"),
        P("user", "tensor"),
        P("user", "tensor"),
        P("user"),
        P("user"),
    )
    out_specs = (P("user", None, "tensor"), P("user", "tensor"), P("user", "tensor"))
    return jax.shard_map(local, mesh=mesh, in_specs=in_specs, out_specs=out_specs, check_vma=False)
```

profile of v0, /device:TPU:8, one launch (start us, length us, event | category | flops | bytes accessed | tf_op | source)
XLA Modules:
  0.0 963.1 jit_solution(14565554388155570690)
XLA Ops:
  7.2 1.4 dynamic-slice
  10.1 19.4 %all-reduce = s32[1024]{0:T(1024)S(1)} all-reduce(s32[1024]{0:T(1024)S(1)} %dynamic-update-slice), channel_id=1, replica_groups=mesh['user'=32,'tensor'=8] {'user'}, use_global_device_ids=true, to_apply=%add | all-reduce | flops 1024 | bytes 8192
  29.6 1.2 broadcast.355.clone
  30.8 5.2 scatter_fusion
  36.0 4.1 all-to-all-start
  40.1 1.2 broadcast.355.clone.1
  41.3 4.6 scatter_fusion.1
  45.9 22.5 %all-to-all-done = bf16[32,128,128]{2,1,0:T(8,128)(2,1)S(1)} async-done(((bf16[32,128,128]{2,1,0:T(8,128)(2,1)}), bf16[32,128,128]{2,1,0:T(8,128)(2,1)S(1)}, u32[]{:S(2)}, u32[]{:S(2)}) %all-to-all-start) | async-done | bytes 1048608 | tf_op jit(solution)/shard_map/all_to_all | solution.py:44
  68.5 4.1 all-to-all-start.1
  73.2 6.2 gather_fusion.2
  79.4 21.5 %all-to-all-done.1 = bf16[32,128,128]{2,1,0:T(8,128)(2,1)S(1)} async-done(((bf16[32,128,128]{2,1,0:T(8,128)(2,1)}), bf16[32,128,128]{2,1,0:T(8,128)(2,1)S(1)}, u32[]{:S(2)}, u32[]{:S(2)}) %all-to-all-start.1) | async-done | bytes 1048608 | tf_op jit(solution)/shard_map/all_to_all | solution.py:43
  100.9 6.2 gather_fusion.3
  107.1 1.3 broadcast_select_fusion.2
  109.2 36.2 %all_gather.17 = bf16[1024,128]{1,0:T(8,128)(2,1)} all-gather(bf16[32,128]{1,0:T(8,128)(2,1)S(1)} %copy-done.43), channel_id=1, replica_groups=mesh['user'=32,'tensor'=8] {'user'}, dimensions={0}, use_global_device_ids=true | all-gather | bytes 270336 | tf_op jit(solution)/shard_map/all_gather | solution.py:55
  145.9 38.0 %all-gather.6.cloned.1.call-done = bf16[2048,1024]{1,0:T(8,128)(2,1)} async-done(((bf16[2048,128]{1,0:T(8,128)(2,1)}), bf16[2048,1024]{1,0:T(8,128)(2,1)}) %all-gather.6.cloned.1.call-update) | async-done | bytes 4194320 | tf_op jit(solution)/shard_map/all_gather | solution.py:51
  183.9 3.0 convert_reduce_fusion
  187.3 1.4 fusion.2
  188.7 59.8 %all-gather.8.cloned.1.call-done = bf16[1024,512]{1,0:T(8,128)(2,1)} async-done(((bf16[32,512]{1,0:T(8,128)(2,1)}), bf16[1024,512]{1,0:T(8,128)(2,1)}) %all-gather.8.cloned.1.call-update) | async-done | bytes 1048592 | tf_op jit(solution)/shard_map/all_gather | solution.py:54
  248.5 6.9 multiply_convert_fusion
  258.2 8.7 select_convert_fusion.5
  272.5 56.3 %all-gather.4.cloned.1.call-done = bf16[2048,1024]{1,0:T(8,128)(2,1)} async-done(((bf16[2048,128]{1,0:T(8,128)(2,1)}), bf16[2048,1024]{1,0:T(8,128)(2,1)}) %all-gather.4.cloned.1.call-update) | async-done | bytes 4194320 | tf_op jit(solution)/shard_map/all_gather | solution.py:52
  328.8 3.9 convolution_bitcast_fusion
  333.3 1.9 fusion.38
  335.7 3.4 select_convert_fusion.3
  340.6 0.9 fusion.37
  341.6 2.9 select_convert_fusion.2
  345.0 1.7 copy-done.3
  346.7 2.9 select_convert_fusion
  350.1 1.1 copy-done.16
  353.4 3.1 select_convert_fusion.1
  360.0 1.9 copy-done.8
  361.9 1.5 fusion.3
  363.4 5.6 fusion.63
  370.1 4.2 convolution_convert_fusion
  374.4 6.2 fusion.10
  380.6 334.5 %all-reduce.3.cloned.1.call-done = f32[2048,1024]{1,0:T(8,128)} async-done(((f32[2048,1024]{1,0:T(8,128)}), f32[2048,1024]{1,0:T(8,128)}) %all-reduce.3.cloned.1.call-update) | async-done | bytes 8388624 | tf_op jit(solution)/shard_map/psum | solution.py:157
  715.1 6.0 fusion.56
  721.1 2.0 add_convert_fusion
  723.2 12.1 %gather_fusion = bf16[4096,128]{1,0:T(8,128)(2,1)S(1)} fusion(bf16[2048,128]{1,0:T(8,128)(2,1)S(1)} %add_convert_fusion, s32[4096]{0:T(1024)S(1)} %broadcast_clamp_fusion), kind=kCustom, calls=%fused_computation.2 | custom fusion | bytes 2113536 | tf_op jit(solution)/shard_map/jit(_take)/gather | solution.py:166
  735.4 1.4 select_select_fusion
  736.8 1.2 broadcast.355
  738.0 4.6 scatter_fusion.2
  742.6 7.4 all-to-all-start.2
  750.0 85.5 %reduce-scatter.5.cloned.1.call-done = bf16[32,128]{1,0:T(8,128)(2,1)} async-done(((bf16[1024,128]{1,0:T(8,128)(2,1)}), bf16[32,128]{1,0:T(8,128)(2,1)}) %reduce-scatter.5.cloned.1.call-update) | async-done | bytes 8208 | tf_op jit(solution)/shard_map/reduce_scatter | solution.py:135
  835.5 1.3 convert_element_type.133
  836.8 115.9 %reduce-scatter.3.cloned.1.call-done = bf16[32,512]{1,0:T(8,128)(2,1)} async-done(((bf16[1024,512]{1,0:T(8,128)(2,1)}), bf16[32,512]{1,0:T(8,128)(2,1)}) %reduce-scatter.3.cloned.1.call-update) | async-done | bytes 32784 | tf_op jit(solution)/shard_map/reduce_scatter | solution.py:144
  952.8 1.4 convert_element_type.127
  954.9 1.1 broadcast_select_fusion
  (226 shorter events, 22.1 us)
Async XLA Ops:
  7.2 34.2 %copy-start.23 = (bf16[32,128,128]{2,1,0:T(8,128)(2,1)S(1)}, bf16[32,128,128]{2,1,0:T(8,128)(2,1)}, u32[]{:S(2)}) copy-start(bf16[32,128,128]{2,1,0:T(8,128)(2,1)} %param.8) | copy-start | bytes 3145732
  29.6 6.5 copy-start.68
  29.6 16.4 %copy-start.46 = (s32[32]{0:T(128)}, s32[32]{0:T(128)S(1)}, u32[]{:S(2)}) copy-start(s32[32]{0:T(128)S(1)} %fusion.52) | copy-start | bytes 388
  36.0 36.6 %copy-start.64 = (s32[32]{0:T(128)S(1)}, s32[32]{0:T(128)}, u32[]{:S(2)}) copy-start(s32[32]{0:T(128)} %param.13) | copy-start | bytes 388
  36.0 37.0 %copy-start.66 = (s32[32]{0:T(128)S(1)}, s32[32]{0:T(128)}, u32[]{:S(2)}) copy-start(s32[32]{0:T(128)} %param.12) | copy-start | bytes 388
  36.0 32.4 %all-to-all-start = ((bf16[32,128,128]{2,1,0:T(8,128)(2,1)}), bf16[32,128,128]{2,1,0:T(8,128)(2,1)S(1)}, u32[]{:S(2)}, u32[]{:S(2)}) async-start(bf16[32,128,128]{2,1,0:T(8,128)(2,1)} %scatter_fusion), calls=%async_computation | async-start | bytes 2097152 | tf_op jit(solution)/shard_map/all_to_all | solution.py:44
  68.5 32.5 %all-to-all-start.1 = ((bf16[32,128,128]{2,1,0:T(8,128)(2,1)}), bf16[32,128,128]{2,1,0:T(8,128)(2,1)S(1)}, u32[]{:S(2)}, u32[]{:S(2)}) async-start(bf16[32,128,128]{2,1,0:T(8,128)(2,1)} %scatter_fusion.1), calls=%async_computation.1 | async-start | bytes 2097152 | tf_op jit(solution)/shard_map/all_to_all | solution.py:43
  72.6 111.3 %all-gather.6.cloned.1.call-start = ((), (), s32[]{:S(2)}) async-start(), calls=%async_computation.6 | async-start | bytes 4718592 | tf_op jit(solution)/shard_map/all_gather | solution.py:51
  72.9 34.2 %copy-start.44 = (s32[32]{0:T(128)}, s32[32]{0:T(128)S(1)}, u32[]{:S(2)}) copy-start(s32[32]{0:T(128)S(1)} %sub.128) | copy-start | bytes 388
  73.0 184.7 %copy-start.27 = (s32[2048]{0:T(1024)}, s32[2048]{0:T(1024)S(1)}, u32[]{:S(2)}) copy-start(s32[2048]{0:T(1024)S(1)} %convert_reduce_fusion.1) | copy-start | bytes 24580
  73.2 184.5 %copy-start.41 = (s32[2048]{0:T(1024)}, s32[2048]{0:T(1024)S(1)}, u32[]{:S(2)}) copy-start(s32[2048]{0:T(1024)S(1)} %get-tuple-element.43) | copy-start | bytes 24580
  79.4 29.8 %copy-start.43 = (bf16[32,128]{1,0:T(8,128)(2,1)S(1)}, bf16[32,128]{1,0:T(8,128)(2,1)}, u32[]{:S(2)}) copy-start(bf16[32,128]{1,0:T(8,128)(2,1)} %param.11) | copy-start | bytes 24580
  108.4 140.1 %all-gather.8.cloned.1.call-start = ((), (), s32[]{:S(2)}) async-start(), calls=%async_computation.7 | async-start | bytes 1081344 | tf_op jit(solution)/shard_map/all_gather | solution.py:54
  109.2 219.7 %all-gather.4.cloned.1.call-start = ((), (), s32[]{:S(2)}) async-start(), calls=%async_computation.5 | async-start | bytes 4718592 | tf_op jit(solution)/shard_map/all_gather | solution.py:52
  145.5 112.3 %copy-start.48 = (s32[512]{0:T(512)}, s32[512]{0:T(512)S(1)}, u32[]{:S(2)}) copy-start(s32[512]{0:T(512)S(1)} %get-tuple-element.35) | copy-start | bytes 6148
  145.5 112.3 %copy-start.50 = (s32[512]{0:T(512)}, s32[512]{0:T(512)S(1)}, u32[]{:S(2)}) copy-start(s32[512]{0:T(512)S(1)} %get-tuple-element.61) | copy-start | bytes 6148
  145.5 112.3 %copy-start.52 = (s32[512]{0:T(512)}, s32[512]{0:T(512)S(1)}, u32[]{:S(2)}) copy-start(s32[512]{0:T(512)S(1)} %get-tuple-element.36) | copy-start | bytes 6148
  145.5 112.3 %copy-start.54 = (s32[512]{0:T(512)}, s32[512]{0:T(512)S(1)}, u32[]{:S(2)}) copy-start(s32[512]{0:T(512)S(1)} %get-tuple-element.60) | copy-start | bytes 6148
  145.5 112.3 %copy-start.56 = (s32[512]{0:T(512)}, s32[512]{0:T(512)S(1)}, u32[]{:S(2)}) copy-start(s32[512]{0:T(512)S(1)} %get-tuple-element.37) | copy-start | bytes 6148
  145.5 112.3 %copy-start.58 = (s32[512]{0:T(512)}, s32[512]{0:T(512)S(1)}, u32[]{:S(2)}) copy-start(s32[512]{0:T(512)S(1)} %get-tuple-element.59) | copy-start | bytes 6148
  145.5 112.3 %copy-start.60 = (s32[512]{0:T(512)}, s32[512]{0:T(512)S(1)}, u32[]{:S(2)}) copy-start(s32[512]{0:T(512)S(1)} %get-tuple-element.38) | copy-start | bytes 6148
  145.5 112.3 %copy-start.62 = (s32[512]{0:T(512)}, s32[512]{0:T(512)S(1)}, u32[]{:S(2)}) copy-start(s32[512]{0:T(512)S(1)} %get-tuple-element.58) | copy-start | bytes 6148
  145.5 569.6 %all-reduce.3.cloned.1.call-start = ((), (), s32[]{:S(2)}) async-start(), calls=%async_computation.8 | async-start | bytes 16777216 | tf_op jit(solution)/shard_map/psum | solution.py:157
  183.9 3.4 copy-start
  257.0 9.9 %copy-start.2 = (f32[512,2048]{1,0:T(8,128)}, f32[512,2048]{1,0:T(8,128)S(1)}, u32[]{:S(2)}) copy-start(f32[512,2048]{1,0:T(8,128)S(1)} %fusion.43) | copy-start | bytes 12582916
  257.8 9.2 copy-start.6
  266.9 3.1 copy-start.17
  266.9 3.9 copy-start.15
  266.9 5.5 copy-start.19
  266.9 5.5 copy-start.21
  267.8 64.9 %copy-start.37 = (f32[512]{0:T(512)}, f32[512]{0:T(512)S(1)}, u32[]{:S(2)}) copy-start(f32[512]{0:T(512)S(1)} %broadcast_multiply_fusion.14) | copy-start | bytes 6148
  268.7 64.2 %copy-start.29 = (f32[512]{0:T(512)}, f32[512]{0:T(512)S(1)}, u32[]{:S(2)}) copy-start(f32[512]{0:T(512)S(1)} %broadcast_multiply_fusion.13) | copy-start | bytes 6148
  270.1 62.9 %copy-start.31 = (f32[512]{0:T(512)}, f32[512]{0:T(512)S(1)}, u32[]{:S(2)}) copy-start(f32[512]{0:T(512)S(1)} %broadcast_multiply_fusion.12) | copy-start | bytes 6148
  271.7 61.6 %copy-start.38 = (f32[512]{0:T(512)}, f32[512]{0:T(512)S(1)}, u32[]{:S(2)}) copy-start(f32[512]{0:T(512)S(1)} %broadcast_multiply_fusion.11) | copy-start | bytes 6148
  272.4 60.8 %copy-start.39 = (f32[512]{0:T(512)}, f32[512]{0:T(512)S(1)}, u32[]{:S(2)}) copy-start(f32[512]{0:T(512)S(1)} %add_rsqrt_fusion.4) | copy-start | bytes 6148
  272.5 60.8 %copy-start.33 = (f32[512]{0:T(512)}, f32[512]{0:T(512)S(1)}, u32[]{:S(2)}) copy-start(f32[512]{0:T(512)S(1)} %add_rsqrt_fusion.3) | copy-start | bytes 6148
  272.5 60.8 %copy-start.35 = (f32[512]{0:T(512)}, f32[512]{0:T(512)S(1)}, u32[]{:S(2)}) copy-start(f32[512]{0:T(512)S(1)} %add_rsqrt_fusion.2) | copy-start | bytes 6148
  272.5 60.8 %copy-start.40 = (f32[512]{0:T(512)}, f32[512]{0:T(512)S(1)}, u32[]{:S(2)}) copy-start(f32[512]{0:T(512)S(1)} %add_rsqrt_fusion.1) | copy-start | bytes 6148
  328.8 3.9 copy-start.14
  328.8 4.1 copy-start.10
  328.8 4.1 copy-start.12
  328.8 6.3 copy-start.22
  369.1 466.4 %reduce-scatter.5.cloned.1.call-start = ((), (), s32[]{:S(2)}) async-start(), calls=%async_computation.10 | async-start | bytes 270336 | tf_op jit(solution)/shard_map/reduce_scatter | solution.py:135
  374.3 578.4 %reduce-scatter.3.cloned.1.call-start = ((), (), s32[]{:S(2)}) async-start(), calls=%async_computation.9 | async-start | bytes 1081344 | tf_op jit(solution)/shard_map/reduce_scatter | solution.py:144
  380.6 340.5 %copy-start.1 = (bf16[2048,128]{1,0:T(8,128)(2,1)S(1)}, bf16[2048,128]{1,0:T(8,128)(2,1)}, u32[]{:S(2)}) copy-start(bf16[2048,128]{1,0:T(8,128)(2,1)} %get-tuple-element.45) | copy-start | bytes 1572868
  735.3 14.6 %copy-start.47 = (s32[32]{0:T(128)S(1)}, s32[32]{0:T(128)}, u32[]{:S(2)}) copy-start(s32[32]{0:T(128)} %copy-done.46) | copy-start | bytes 388
  735.3 14.6 %copy-start.69 = (s32[32]{0:T(128)S(1)}, s32[32]{0:T(128)}, u32[]{:S(2)}) copy-start(s32[32]{0:T(128)} %copy-done.68) | copy-start | bytes 388
  742.6 211.6 %all-to-all-start.2 = ((bf16[32,128,128]{2,1,0:T(8,128)(2,1)}), bf16[32,128,128]{2,1,0:T(8,128)(2,1)S(1)}, u32[]{:S(2)}, u32[]{:S(2)}) async-start(bf16[32,128,128]{2,1,0:T(8,128)(2,1)} %scatter_fusion.2), calls=%async_computation.2 | async-start | bytes 2097152 | tf_op jit(solution)/shard_map/all_to_all | solution.py:169
  (33 other events, 59.5 us)
Sparse Core Ops, SparseCore 0:
  108.5 75.2 all-gather.5
  185.7 62.7 all-gather.7
  251.6 77.1 all-gather.3
  369.2 345.8 all-reduce.2
  717.5 118.0 reduce-scatter.4
  838.0 114.6 reduce-scatter.2
where the time goes:
time: 968 us; the launch traced here: 963 us
  waiting for transfers between devices  735 us (76%)
  matrix products  60.4 us (6%)
  blocking collectives  55.6 us (6%)
  local copies, waits for them, and re-layouts  54.9 us (6%)
  other arithmetic  24.9 us (3%)
  between operations  16.3 us (2%)
  starting transfers between devices  16.1 us (2%)
    psum x1, waiting for transfers between devices, local(): dn_all = lax.psum(dn, 'tensor')  334 us
    reduce_scatter x1, waiting for transfers between devices, local(): lax.psum_scatter(lax.dot_general(columns, dz, (((0,), (0,)), ((), ())), p...  116 us
    reduce_scatter x1, waiting for transfers between devices, local(): lax.psum_scatter(lax.dot_general(columns, hb, (((0,), (0,)), ((), ())), p...  85.5 us
    all_gather x1, waiting for transfers between devices, local(): w_in_cols = lax.all_gather(w_in, 'user', axis=0, tiled=True)  59.8 us
    all_gather x1, waiting for transfers between devices, local(): lax.all_gather(dp, 'tensor', axis=1, tiled=True)  56.3 us
    all_gather x1, waiting for transfers between devices, local(): lax.all_gather(xp, 'tensor', axis=1, tiled=True)  38 us
    all_gather x1, blocking collectives, local(): w_out_cols = lax.all_gather(w_out, 'user', axis=0, tiled=True)  36.2 us
    all_to_all x1, waiting for transfers between devices, local(): lax.all_to_all(send_d, 'user', split_axis=0, concat_axis=0, tiled=True)  22.5 us
  transfers between devices with their start and end apart: 9, of which 8 were waited for; matrix products, arithmetic and copies ran while one was open for 8% of the time, Pallas kernels for 0%

commit v1 on v0

v1 whole, which is shorter than its diff:
```python
import functools

import jax
import jax.numpy as jnp
from jax import lax
from jax.experimental import pallas as pl
from jax.experimental.pallas import tpu as pltpu
from jax.sharding import PartitionSpec as P

MESH = pl.DeviceIdType.MESH
F32 = jnp.float32
BF16 = jnp.bfloat16
EPS = 1e-05
HD = 128
SEQ = 128
HEADS = 8
NX, NY, NZ = 4, 4, 8
HIST = 4
ROWS = HIST * SEQ
D = 1024

COLOURS = ((2, NZ, NX * NY, 384), (0, NX, NY * NZ, 128), (1, NY, NX * NZ, 128))


def place():
    u = lax.axis_index("user")
    t = lax.axis_index("tensor")
    c = lax.rem(u, 2)
    z = lax.rem(u // 2, NZ)
    x = lax.rem(t, 2) * 2 + u // (2 * NZ)
    y = t // 2
    return u, t, c, (x, y, z)


def device_of(x, y, z, c):
    return ((lax.rem(x, 2) * NZ + z) * 2 + c, y * 2 + x // 2)


def ring_and_plane(colour, pos):
    x, y, z = pos
    return ((z, y * NX + x), (x, y * NZ + z), (y, x * NZ + z))[colour]


def plane_device(colour, pos, p, c):
    x, y, z = pos
    if colour == 0:
        return device_of(lax.rem(p, NX), p // NX, z, c)
    if colour == 1:
        return device_of(x, p // NZ, lax.rem(p, NZ), c)
    return device_of(p // NZ, y, lax.rem(p, NZ), c)


def ring_device(colour, pos, step, c):
    axis, n = COLOURS[colour][:2]
    pos = list(pos)
    pos[axis] = lax.rem(pos[axis] + step + n, n)
    return device_of(*pos, c)


def remote(src, dst, send, recv, device):
    return pltpu.make_async_remote_copy(
        src_ref=src, dst_ref=dst, send_sem=send, recv_sem=recv, device_id=device, device_id_type=MESH
    )


def wait_bytes(ref, sem):
    pltpu.make_async_copy(ref, ref, sem).wait()


def gather_kernel(
    ev, ct, w_in, w_out, tab, gz, gx, gy, xr, dr, tabs,
    bounce, plane_send, plane_recv, rs, rr, fwd_send, fwd_recv, a2a_send, a2a_recv, tab_send, tab_recv, loc,
):
    u, t, c, pos = place()
    gs = (gz, gx, gy)
    pieces = (w_in.at[:, pl.ds(0, 384)], w_in.at[:, pl.ds(384, 128)], w_out)
    partner = (u + 1 - 2 * c, t)
    locals_ = []

    for col in (1, 2, 0):
        n, m = COLOURS[col][1:3]
        a, p = ring_and_plane(col, pos)
        own = pltpu.make_async_copy(pieces[col], gs[col].at[c, a, p], loc.at[col])
        own.start()
        locals_.append(own)

        @pl.loop(1, m)
        def _(i):
            q = lax.rem(p + i, m)
            remote(
                pieces[col], gs[col].at[c, a, p], plane_send.at[col], plane_recv.at[col],
                plane_device(col, pos, q, c),
            ).start()

    @pl.loop(1, HEADS)
    def _(i):
        q = lax.rem(t + i, HEADS)
        for k, (src, dst) in enumerate(((ev, xr), (ct, dr))):
            remote(src.at[pl.ds(q * HIST, HIST)], dst.at[t], a2a_send.at[k], a2a_recv.at[k], (u, q)).start()

    ins = []
    for k, src in enumerate((ev, ct)):
        copy = pltpu.make_async_copy(src.at[pl.ds(t * HIST, HIST)], bounce.at[k], loc.at[3 + k])
        copy.start()
        ins.append(copy)

    @pl.loop(1, 32)
    def _(i):
        remote(tab, tabs.at[u], tab_send, tab_recv, (lax.rem(u + i, 32), t)).start()

    own_tab = pltpu.make_async_copy(tab, tabs.at[u], loc.at[5])
    own_tab.start()
    for k, dst in enumerate((xr, dr)):
        ins[k].wait()
        copy = pltpu.make_async_copy(bounce.at[k], dst.at[t], loc.at[6 + k])
        copy.start()
        locals_.append(copy)
    locals_.append(own_tab)
    for copy in locals_:
        copy.wait()

    sends = []

    def sem_index(col, direction, k, half):
        base = (0, 16, 24)[col]
        return base + (direction * (COLOURS[col][1] // 2) + k) * 2 + half

    def halves(col, k, direction):
        if k == COLOURS[col][1] // 2 - 1:
            return (direction,)
        return (0, 1)

    def block(col, idx, half):
        m = COLOURS[col][2]
        return gs[col].at[c, idx, pl.ds(half * (m // 2), m // 2)]

    def forward(col, idx, half):
        part = block(col, idx, half)
        remote(part, part, fwd_send.at[col], fwd_recv.at[col], partner).start()

    def ring_send(col, k, direction, half):
        n = COLOURS[col][1]
        a, _ = ring_and_plane(col, pos)
        step = 1 - 2 * direction
        part = block(col, lax.rem(a - step * k + n, n), half)
        s = sem_index(col, direction, k, half)
        copy = remote(part, part, rs.at[s], rr.at[s], ring_device(col, pos, step, c))
        copy.start()
        sends.append(copy)

    def ring_wait(col, k, direction, half):
        n = COLOURS[col][1]
        a, _ = ring_and_plane(col, pos)
        step = 1 - 2 * direction
        idx = lax.rem(a - step * (k + 1) + n, n)
        s = sem_index(col, direction, k, half)
        wait_bytes(block(col, idx, half), rr.at[s])
        forward(col, idx, half)

    for col in (1, 2, 0):
        m = COLOURS[col][2]
        a, p = ring_and_plane(col, pos)
        wait_bytes(gs[col].at[c, a, pl.ds(0, m - 1)], plane_recv.at[col])
        for half in (0, 1):
            for direction in (0, 1):
                if half in halves(col, 0, direction):
                    ring_send(col, 0, direction, half)
        for half in (0, 1):
            forward(col, a, half)

    for k in range(NZ // 2):
        for col in (1, 2, 0):
            if k >= COLOURS[col][1] // 2:
                continue
            for half in (0, 1):
                for direction in (0, 1):
                    if half in halves(col, k, direction):
                        ring_wait(col, k, direction, half)
                        if k + 1 < COLOURS[col][1] // 2 and half in halves(col, k + 1, direction):
                            ring_send(col, k + 1, direction, half)

    for copy in sends:
        copy.wait_send()
    for col in range(3):
        m = COLOURS[col][2]
        a, p = ring_and_plane(col, pos)
        wait_bytes(gs[col].at[c, a, pl.ds(0, m - 1)], plane_send.at[col])
        wait_bytes(gs[col].at[c], fwd_send.at[col])
        wait_bytes(gs[col].at[1 - c], fwd_recv.at[col])
    for k, ref in enumerate((xr, dr)):
        wait_bytes(ref.at[pl.ds(0, HEADS - 1)], a2a_send.at[k])
        wait_bytes(ref.at[pl.ds(0, HEADS - 1)], a2a_recv.at[k])
    wait_bytes(tabs.at[pl.ds(0, 31)], tab_send)
    wait_bytes(tabs.at[pl.ds(0, 31)], tab_recv)


def gather(events, cotangent, w_in, w_out, tab):
    any_ = pl.BlockSpec(memory_space=pl.ANY)
    vmem = pl.BlockSpec(memory_space=pltpu.VMEM)
    shape = jax.ShapeDtypeStruct
    out_shape = tuple(shape((2, n, m, 32, w), BF16) for _, n, m, w in COLOURS) + (
        shape((HEADS, HIST, SEQ, 128), BF16),
        shape((HEADS, HIST, SEQ, 128), BF16),
        shape((32, 8, 128), jnp.int32),
    )
    dma = pltpu.SemaphoreType.DMA
    return pl.pallas_call(
        gather_kernel,
        out_shape=out_shape,
        in_specs=[any_, any_, vmem, vmem, any_],
        out_specs=(any_,) * 6,
        scratch_shapes=[
            pltpu.VMEM((2, HIST, SEQ, 128), BF16),
            dma((3,)), dma((3,)), dma((32,)), dma((32,)), dma((3,)), dma((3,)),
            dma((2,)), dma((2,)), dma, dma, dma((8,)),
        ],
        compiler_params=pltpu.CompilerParams(has_side_effects=True),
        name="gather",
    )(events, cotangent, w_in, w_out, tab)


def silu_parts(v):
    sig = jax.nn.sigmoid(v)
    return v * sig, sig * (1.0 + v * (1.0 - sig))


def dot(a, b, dims):
    return lax.dot_general(a, b, (dims, ((), ())), preferred_element_type=F32)


NN, NT, TN = ((1,), (0,)), ((1,), (1,)), ((0,), (0,))


def layer_kernel(
    xr, dr, tabs, gz, gx, gy, pz, px, py, dxr,
    nf, nb, nbt, dm, dmt, rstd_s, dn, wh, wo, dz_s, hb_s,
):
    h = pl.program_id(0)

    @pl.when(h == 0)
    def _():
        u = lax.axis_index("user")
        t = lax.axis_index("tensor")
        lens = jnp.sum(jnp.where(tabs[:, 0, :] == u, tabs[:, 1, :], 0).astype(F32), axis=0, keepdims=True)
        lane = lax.broadcasted_iota(jnp.int32, (1, 128), 1)
        for i in range(HIST):
            rows = pl.ds(i * SEQ, SEQ)
            xs = jnp.concatenate([xr[k, i] for k in range(HEADS)], axis=1).astype(F32)
            cen = xs - jnp.mean(xs, axis=1, keepdims=True)
            rstd = lax.rsqrt(jnp.mean(cen * cen, axis=1, keepdims=True) + EPS)
            nfi = cen * rstd
            nf[rows, :] = nfi
            rstd_s[rows, :] = jnp.broadcast_to(rstd, (SEQ, 128))
            nbi = nfi.astype(BF16)
            nb[rows, :] = nbi
            nbt[:, rows] = nbi.T
            length = jnp.sum(jnp.where(lane == t * HIST + i, lens, 0.0), axis=1, keepdims=True)
            pos = lax.broadcasted_iota(jnp.int32, (SEQ, D), 0).astype(F32)
            ds_ = jnp.concatenate([dr[k, i] for k in range(HEADS)], axis=1).astype(F32)
            di = jnp.where(pos < length, ds_, 0.0).astype(BF16)
            dm[rows, :] = di
            dmt[:, rows] = di.T
        dn[...] = jnp.zeros_like(dn)

    for xl in range(2):
        for z in range(NZ):
            for c in range(2):
                r = pl.ds(((xl * NZ + z) * 2 + c) * 32, 32)
                wh[r, pl.ds(0, 384)] = gz[c, z, 0, xl]
                wh[r, pl.ds(384, 128)] = gx[c, 0, xl, 0, z]
                wo[r, :] = gy[c, 0, xl, z]

    scale = HD ** (-0.5)
    causal = lax.broadcasted_iota(jnp.int32, (SEQ, SEQ), 1) <= lax.broadcasted_iota(jnp.int32, (SEQ, SEQ), 0)
    for i in range(HIST):
        rows = pl.ds(i * SEQ, SEQ)
        zi = dot(nb[rows, :], wh[...], NN)
        gi, sgi = silu_parts(zi)
        gi = gi.astype(BF16)
        grad_h = dot(dm[rows, :], wo[...], NN)
        uf = gi[:, 0:128].astype(F32)
        vp, qp, kp = gi[:, 128:256], gi[:, 256:384], gi[:, 384:512]
        s = dot(qp, kp, NT) * scale
        ss, sgs = silu_parts(s)
        at = jnp.where(causal, ss / SEQ, 0.0).astype(BF16)
        yv = dot(at, vp, NN)
        ycen = yv - jnp.mean(yv, axis=1, keepdims=True)
        yrstd = lax.rsqrt(jnp.mean(ycen * ycen, axis=1, keepdims=True) + EPS)
        yn = ycen * yrstd
        hb_s[rows, :] = (yn * uf).astype(BF16)
        grad_u = grad_h * yn
        gyn = grad_h * uf
        dy = (
            (gyn - jnp.mean(gyn, axis=1, keepdims=True) - yn * jnp.mean(gyn * yn, axis=1, keepdims=True)) * yrstd
        ).astype(BF16)
        da = dot(dy, vp, NT)
        grad_v = dot(at, dy, TN)
        ds_ = jnp.where(causal, da * sgs * (scale / SEQ), 0.0).astype(BF16)
        grad_q = dot(ds_, kp, NN)
        grad_k = dot(ds_, qp, TN)
        dz_s[rows, :] = (jnp.concatenate([grad_u, grad_v, grad_q, grad_k], axis=1) * sgi).astype(BF16)

    for j in range(4):
        gw = dot(nbt[pl.ds(j * 256, 256), :], dz_s[...], NN).astype(BF16)
        go = dot(dmt[pl.ds(j * 256, 256), :], hb_s[...], NN).astype(BF16)
        for k in range(8):
            uu = j * 8 + k
            c, z, xl = uu % 2, (uu // 2) % NZ, uu // (2 * NZ)
            pz[c, z, 0, xl] = gw[k * 32 : k * 32 + 32, 0:384]
            px[c, 0, xl, 0, z] = gw[k * 32 : k * 32 + 32, 384:512]
            py[c, 0, xl, z] = go[k * 32 : k * 32 + 32, :]
        dn[:, pl.ds(j * 256, 256)] += dot(dz_s[...], wh[pl.ds(j * 256, 256), :], NT)

    @pl.when(h == HEADS - 1)
    def _():
        for i in range(HIST):
            rows = pl.ds(i * SEQ, SEQ)
            dni, nfi = dn[rows, :], nf[rows, :]
            branch = (
                dni - jnp.mean(dni, axis=1, keepdims=True) - nfi * jnp.mean(dni * nfi, axis=1, keepdims=True)
            ) * rstd_s[rows, 0:1]
            out = (dm[rows, :].astype(F32) + branch).astype(BF16)
            for k in range(HEADS):
                dxr[k, i] = out[:, k * 128 : k * 128 + 128]


def layer(xr, dr, tabs, gz, gx, gy):
    full = lambda shape: pl.BlockSpec(shape, lambda h: (0,) * len(shape), pipeline_mode=pl.Buffered(1))
    zspec = pl.BlockSpec((2, NZ, 1, 2, 32, 384), lambda h: (0, 0, h, 0, 0, 0))
    xspec = pl.BlockSpec((2, 1, 2, 1, NZ, 32, 128), lambda h: (0, lax.rem(h, 2), 0, h // 2, 0, 0, 0))
    yspec = pl.BlockSpec((2, 1, 2, NZ, 32, 128), lambda h: (0, h, 0, 0, 0, 0))
    zs, xs, ys = (2, NZ, HEADS, 2, 32, 384), (2, 2, 2, NY, NZ, 32, 128), (2, HEADS, 2, NZ, 32, 128)
    shape = jax.ShapeDtypeStruct
    rows = (HEADS, HIST, SEQ, 128)
    pz, px, py, dxr = pl.pallas_call(
        layer_kernel,
        grid=(HEADS,),
        out_shape=(shape(zs, BF16), shape(xs, BF16), shape(ys, BF16), shape(rows, BF16)),
        in_specs=[full(rows), full(rows), full((32, 8, 128)), zspec, xspec, yspec],
        out_specs=(zspec, xspec, yspec, pl.BlockSpec(rows, lambda h: (0,) * 4)),
        scratch_shapes=[
            pltpu.VMEM((ROWS, D), F32),
            pltpu.VMEM((ROWS, D), BF16),
            pltpu.VMEM((D, ROWS), BF16),
            pltpu.VMEM((ROWS, D), BF16),
            pltpu.VMEM((D, ROWS), BF16),
            pltpu.VMEM((ROWS, 128), F32),
            pltpu.VMEM((ROWS, D), F32),
            pltpu.VMEM((D, 512), BF16),
            pltpu.VMEM((D, 128), BF16),
            pltpu.VMEM((ROWS, 512), BF16),
            pltpu.VMEM((ROWS, 128), BF16),
        ],
        compiler_params=pltpu.CompilerParams(
            dimension_semantics=("arbitrary",), vmem_limit_bytes=56 * 1024 * 1024
        ),
        name="layer",
    )(xr, dr, tabs, gz.reshape(zs), gx.reshape(xs), gy.reshape(ys))
    return [p.reshape((2, n, m, 32, w)) for p, (_, n, m, w) in zip((pz, px, py), COLOURS)] + [dxr]


def scatter_kernel(
    pz, px, py, dxr, grad_x, grad_wi, grad_wo,
    az, ax, ay, bz, bx, by, rz, rx, ry, qz, qx, qy, bounce,
    par_send, par_recv, ld, rs, rr, plane_send, plane_recv, a2a_send, a2a_recv, loc,
):
    u, t, c, pos = place()
    partner = (u + 1 - 2 * c, t)
    ps, accs, theirs, rings, planes = (pz, px, py), (az, ax, ay), (bz, bx, by), (rz, rx, ry), (qz, qx, qy)

    def block_sem(col, idx, half):
        return (0, 16, 24)[col] + idx * 2 + half

    def part(ref, col, idx, half):
        m = COLOURS[col][2]
        return ref.at[idx, pl.ds(half * (m // 2), m // 2)]

    def order(col, j):
        n = COLOURS[col][1]
        return (n // 2 - j, j - n // 2)

    def offsets(col):
        n = COLOURS[col][1]
        out = []
        for j in range(n // 2 + 1):
            for o in order(col, j):
                if o % n not in out:
                    out.append(o % n)
        return out

    def index(col, off):
        n = COLOURS[col][1]
        a, _ = ring_and_plane(col, pos)
        return lax.rem(a + off + n, n)

    def start_block(col, off):
        idx = index(col, off)
        m = COLOURS[col][2]
        for half in (0, 1):
            s = (0, 16, 24)[col] + (off % COLOURS[col][1]) * 2 + half
            sub = pl.ds(half * (m // 2), m // 2)
            remote(
                ps[col].at[1 - c, idx, sub], part(theirs[col], col, idx, half), par_send.at[s], par_recv.at[s], partner
            ).start()
            pltpu.make_async_copy(ps[col].at[c, idx, sub], part(accs[col], col, idx, half), ld.at[s]).start()

    for j in range(NZ // 2 + 1):
        for col in (0, 1, 2):
            n = COLOURS[col][1]
            if j > n // 2:
                continue
            offs = sorted({o % n for o in order(col, j)})
            for off in offs:
                start_block(col, off)

    ins = pltpu.make_async_copy(dxr.at[t], bounce, loc.at[0])
    ins.start()

    @pl.loop(1, HEADS)
    def _(i):
        q = lax.rem(t + i, HEADS)
        remote(dxr.at[q], grad_x.at[pl.ds(t * HIST, HIST)], a2a_send, a2a_recv, (u, q)).start()

    ins.wait()
    own = pltpu.make_async_copy(bounce, grad_x.at[pl.ds(t * HIST, HIST)], loc.at[1])
    own.start()

    def ring_slot(col, k, direction, half):
        n = COLOURS[col][1]
        return (direction * (n // 2) + k) * 2 + half

    sends = []

    def add(col, off, half, slots):
        idx = index(col, off)
        m = COLOURS[col][2]
        s = (0, 16, 24)[col] + (off % COLOURS[col][1]) * 2 + half
        mine = part(accs[col], col, idx, half)
        other = part(theirs[col], col, idx, half)
        wait_bytes(mine, ld.at[s])
        wait_bytes(other, par_recv.at[s])
        got = []
        for k, direction in slots:
            slot = ring_slot(col, k, direction, half)
            ref = rings[col].at[slot]
            wait_bytes(ref, rr.at[(0, 16, 24)[col] + slot])
            got.append(ref)

        @pl.loop(0, m // 2)
        def _(i):
            v = mine[i].astype(F32) + other[i].astype(F32)
            for ref in got:
                v = v + ref[i].astype(F32)
            mine[i] = v.astype(BF16)

    def ring_send(col, k, direction, half, off):
        idx = index(col, off)
        slot = ring_slot(col, k, direction, half)
        s = (0, 16, 24)[col] + slot
        copy = remote(
            part(accs[col], col, idx, half), rings[col].at[slot], rs.at[s], rr.at[s],
            ring_device(col, pos, 1 - 2 * direction, c),
        )
        copy.start()
        sends.append(copy)

    for k in range(NZ // 2):
        for col in (1, 2, 0):
            n = COLOURS[col][1]
            if k >= n // 2:
                continue
            for half in (0, 1):
                for direction in (0, 1):
                    off = order(col, k)[direction]
                    if k == 0:
                        if half == direction:
                            add(col, off, half, ())
                            ring_send(col, k, direction, half, off)
                        continue
                    slots = ((k - 1, direction),) if (k > 1 or half == direction) else ()
                    add(col, off, half, slots)
                    ring_send(col, k, direction, half, off)

    for col in (1, 2, 0):
        n, m, w = COLOURS[col][1:]
        a, p = ring_and_plane(col, pos)
        for half in (0, 1):
            k = n // 2 - 1
            slots = tuple((k, d) for d in (0, 1))
            add(col, 0, half, slots)

        @pl.loop(1, m)
        def _(i):
            q = lax.rem(p + i, m)
            remote(
                accs[col].at[a, q], planes[col].at[p], plane_send.at[col], plane_recv.at[col],
                plane_device(col, pos, q, c),
            ).start()

    outs = (grad_wi.at[:, pl.ds(0, 384)], grad_wi.at[:, pl.ds(384, 128)], grad_wo)
    for col in (1, 2, 0):
        n, m, w = COLOURS[col][1:]
        a, p = ring_and_plane(col, pos)
        wait_bytes(planes[col].at[pl.ds(0, m - 1)], plane_recv.at[col])
        mine = accs[col].at[a, p]

        def body(i, total):
            return total + planes[col][lax.rem(p + i, m)].astype(F32)

        outs[col][...] = lax.fori_loop(1, m, body, mine[...].astype(F32))

    for copy in sends:
        copy.wait_send()
    for col in range(3):
        n, m, w = COLOURS[col][1:]
        wait_bytes(planes[col].at[pl.ds(0, m - 1)], plane_send.at[col])
        for off in range(n):
            for half in (0, 1):
                s = (0, 16, 24)[col] + off * 2 + half
                wait_bytes(part(theirs[col], col, index(col, off), half), par_send.at[s])
    own.wait()
    wait_bytes(dxr.at[pl.ds(0, HEADS - 1)], a2a_send)
    wait_bytes(dxr.at[pl.ds(0, HEADS - 1)], a2a_recv)


def scatter(pz, px, py, dxr):
    any_ = pl.BlockSpec(memory_space=pl.ANY)
    vmem = pl.BlockSpec(memory_space=pltpu.VMEM)
    shape = jax.ShapeDtypeStruct
    dma = pltpu.SemaphoreType.DMA
    blocks = [pltpu.VMEM((n, m, 32, w), BF16) for _, n, m, w in COLOURS]
    rings = [pltpu.VMEM((2 * n, m // 2, 32, w), BF16) for _, n, m, w in COLOURS]
    planes = [pltpu.VMEM((m, 32, w), BF16) for _, n, m, w in COLOURS]
    return pl.pallas_call(
        scatter_kernel,
        out_shape=(shape((32, SEQ, 128), BF16), shape((32, 512), F32), shape((32, 128), F32)),
        in_specs=[any_] * 4,
        out_specs=(any_, vmem, vmem),
        scratch_shapes=blocks + blocks + rings + planes + [
            pltpu.VMEM((HIST, SEQ, 128), BF16),
            dma((32,)), dma((32,)), dma((32,)), dma((32,)), dma((32,)), dma((3,)), dma((3,)), dma, dma, dma((2,)),
        ],
        compiler_params=pltpu.CompilerParams(has_side_effects=True, vmem_limit_bytes=48 * 1024 * 1024),
        name="scatter",
    )(pz, px, py, dxr)


def local(events, cotangent, w_in, w_out, slot_source, slot_length):
    tab = jnp.full((8, 128), -1, jnp.int32).at[0, :32].set(slot_source).at[1, :32].set(slot_length)
    gz, gx, gy, xr, dr, tabs = gather(events, cotangent, w_in, w_out, tab)
    pz, px, py, dxr = layer(xr, dr, tabs, gz, gx, gy)
    return scatter(pz, px, py, dxr)


def solution(mesh):
    in_specs = (
        P("user", None, "tensor"),
        P("user", None, "tensor"),
        P("user", "tensor"),
        P("user", "tensor"),
        P("user"),
        P("user"),
    )
    out_specs = (P("user", None, "tensor"), P("user", "tensor"), P("user", "tensor"))
    return jax.shard_map(local, mesh=mesh, in_specs=in_specs, out_specs=out_specs, check_vma=False)
```

time: 968 us -> 219 us (0.23)
  waiting for transfers between devices: 735 us -> 0 us
  Pallas kernels: 0 us -> 211 us
  matrix products: 60.4 us -> 0 us
  blocking collectives: 55.6 us -> 0 us
  local copies, waits for them, and re-layouts: 54.9 us -> 7.01 us
  other arithmetic: 24.9 us -> 0 us
  starting transfers between devices: 16.1 us -> 0 us
  between operations: 16.3 us -> 0.67 us
    psum x1 -> x0, waiting for transfers between devices: 334 us -> none  [local(): dn_all = lax.psum(dn, 'tensor')]
    pallas_call x0 -> x3, Pallas kernels: none -> 211 us  [the longest x1 83 us: gather(): pl.pallas_call(gather_kernel, out_shape=out_shape, in_specs=[any_, any_,...]
    reduce_scatter x2 -> x0, waiting for transfers between devices: 201 us -> none  [the longest x1 116 us: local(): lax.psum_scatter(lax.dot_general(columns, dz, (((0,), (0,)), ((), ())), p...]
    all_gather x3 -> x0, waiting for transfers between devices: 154 us -> none  [the longest x1 59.8 us: local(): w_in_cols = lax.all_gather(w_in, 'user', axis=0, tiled=True)]
    dot_general x29 -> x0, matrix products: 60.4 us -> none  [the longest x4 12.3 us: local(): jnp.einsum('hqe,hke->hqk', grad_y, vpart, preferred_element_type=jnp.floa...]
    all_to_all x3 -> x0, waiting for transfers between devices: 44 us -> none  [the longest x1 22.5 us: local(): lax.all_to_all(send_d, 'user', split_axis=0, concat_axis=0, tiled=True)]
    all_gather x1 -> x0, blocking collectives: 36.2 us -> none  [local(): w_out_cols = lax.all_gather(w_out, 'user', axis=0, tiled=True)]
    gather x4 -> x0, local copies, waits for them, and re-layouts: 25.2 us -> none  [the longest x1 12.1 us: local(): jnp.take(dxp, rows_at.reshape(-1), axis=0)]
  transfers between devices with their start and end apart: 9 -> 0, of which waited for: 8 -> 0; matrix products, arithmetic and copies ran while one was open for 8% -> 0% of each run, Pallas kernels for 0% -> 0%
where the time goes in v1:
time: 219 us; the launch traced here: 218 us
  Pallas kernels  211 us (96%)
  local copies, waits for them, and re-layouts  7.01 us (3%)
    pallas_call x1, Pallas kernels, gather(): pl.pallas_call(gather_kernel, out_shape=out_shape, in_specs=[any_, any_,...  83 us
    pallas_call x1, Pallas kernels, scatter(): pl.pallas_call(scatter_kernel, out_shape=(shape((32, SEQ, 128), BF16), sh...  76.8 us
    pallas_call x1, Pallas kernels, layer(): pl.pallas_call(layer_kernel, grid=(HEADS,), out_shape=(shape(zs, BF16), s...  50.8 us
    unnamed x9, local copies, waits for them, and re-layouts  5.6 us

profile of v1, /device:TPU:8, one launch (start us, length us, event | category | flops | bytes accessed | tf_op | source)
XLA Modules:
  0.0 218.3 jit_solution(14106953709552217504)
XLA Ops:
  0.6 0.7 scatter.9
  1.3 0.7 scatter.12.tab
  2.0 0.0 copy-start.2
  2.0 0.6 copy-done.2
  2.6 83.0 %gather.1 = (bf16[2,8,16,32,384]{4,3,2,1,0:T(8,128)(2,1)}, bf16[2,4,32,32,128]{4,3,2,1,0:T(8,128)(2,1)}, bf16[2,4,32,32,128]{4,3,2,1,0:T(8,128)(2,1)}, bf16[8,4,...) custom-call(bf16[32,128,128]{2,1,0:T(8,128)(2,1)} %ev.1, ...), custom_call_target="tpu_custom_call" | custom-call | tf_op jit(solution)/shard_map/gather/pallas_call | solution.py:207
  85.7 50.8 %layer.1 = (bf16[2,8,8,2,32,384]{5,4,3,2,1,0:T(8,128)(2,1)}, bf16[2,2,2,4,8,32,128]{6,5,4,3,2,1,0:T(8,128)(2,1)}, bf16[2,8,2,8,32,128]{5,4,3,2,1,0:T(8,128)(2,1)}, bf16[8,4,128,128]{3,2,1,0:T(8,128)(2,1)}) custom-call(bf16[8,4,128,128]{3,2,1,0:T(8,128)(2,1)} %get-tuple-element.37.xr, bf16[8,4,128,128]{3,2,1,0:T(8,128)(2,1)} %get-tuple-element.38.dr, ...), custom_call_target="tpu_custom_call" | custom-call | tf_op jit(solution)/shard_map/layer/pallas_call | solution.py:335
  136.5 0.0 copy-start
  136.5 1.6 copy-done
  138.1 0.0 copy-start.1
  138.1 1.2 copy-done.1
  139.3 76.8 %scatter.13 = (bf16[32,128,128]{2,1,0:T(8,128)(2,1)S(1)}, f32[32,512]{1,0:T(8,128)S(1)}, f32[32,128]{1,0:T(8,128)S(1)}) custom-call(bf16[2,8,16,32,384]{4,3,2,1,0:T(8,128)(2,1)} %bitcast.10, bf16[2,4,32,32,128]{4,3,2,1,0:T(8,128)(2,1)S(1)} %bitcast.8, bf16[2,4,32,32,128]{4,3,2,1,0:T(8,128)(2,1)} %bitcast.13, bf16[8,4,128,128]{3,2,1,0:T(8,128)(2,1)S(1)} %copy-done.1), custom_call_target="tpu_custom_call" | custom-call | tf_op jit(solution)/shard_map/scatter/pallas_call | solution.py:534
  216.1 1.0 copy.13
  217.1 0.6 copy.14
  217.7 0.6 copy.15
Async XLA Ops:
  2.0 0.6 copy-start.2
  136.5 1.6 copy-start
  138.1 1.2 copy-start.1

commit v2 on v0

v2 whole, which is shorter than its diff:
```python
import jax
import jax.numpy as jnp
from jax import lax
from jax.experimental import pallas as pl
from jax.experimental.pallas import tpu as pltpu
from jax.sharding import PartitionSpec as P

MESH = pl.DeviceIdType.MESH
F32 = jnp.float32
BF16 = jnp.bfloat16
EPS = 1e-05
HD = 128
SEQ = 128
HEADS = 8
NX, NY, NZ = 4, 4, 8
HIST = 4
ROWS = HIST * SEQ
D = 1024

COLOURS = ((2, NZ, 8, 384), (0, NX, 16, 128), (1, NY, 16, 128))
ORDER = (1, 2, 0)
BASE = (0, 16, 24)


def device_of(x, y, z, c):
    return ((lax.rem(x, 2) * NZ + z) * 2 + c, y * 2 + x // 2)


def remote(src, dst, send, recv, device):
    return pltpu.make_async_remote_copy(
        src_ref=src, dst_ref=dst, send_sem=send, recv_sem=recv, device_id=device, device_id_type=MESH
    )


def wait_bytes(ref, sem):
    pltpu.make_async_copy(ref, ref, sem).wait()


def silu_parts(v):
    sig = jax.nn.sigmoid(v)
    return v * sig, sig * (1.0 + v * (1.0 - sig))


def dot(a, b, dims):
    return lax.dot_general(a, b, (dims, ((), ())), preferred_element_type=F32)


NN, NT, TN = ((1,), (0,)), ((1,), (1,)), ((0,), (0,))


def when(cond, f):
    if isinstance(cond, bool):
        if cond:
            f()
    else:
        pl.when(cond)(f)


def kernel(
    ev, ct, w_in, w_out, tab, grad_x, grad_wi, grad_wo,
    gz, gx, gy, pz, px, py, tz, tx, ty, rz, rx, ry, s1z, s1x, s1y, s2z, s2x, s2y,
    xr, dr, tabs, nf, nb, nbt, dm, dmt, rstd_s, dn, wh, wo, dz_s, hb_s,
    loc, st1_send, st1_recv, st2_send, z2_send, z2_recv, x2_recv, y2_recv, ag_send, ag_recv, fw_send, fw_recv,
    a2a_send, a2a_recv, tab_send, tab_recv, par_send, par_recv, rs_send, rs_recv,
    o1_send, o1z_send, o1_recv, o1z_recv, o2_send, o2_recv, out_send, out_recv,
):
    u = lax.axis_index("user")
    t = lax.axis_index("tensor")
    c = lax.rem(u, 2)
    z = lax.rem(u // 2, NZ)
    x_lo = u // (2 * NZ)
    x_hi = lax.rem(t, 2)
    y = t // 2
    x = x_hi * 2 + x_lo
    mine = lax.rem(y + x_hi, 2)
    partner = (u + 1 - 2 * c, t)
    gs, ps, ts, rings = (gz, gx, gy), (pz, px, py), (tz, tx, ty), (rz, rx, ry)
    place = (z, x, y)

    def x_peer(i):
        return lax.rem(x + i, NX)

    def y_peer(i):
        return lax.rem(y + i, NY)

    def z_peer(i):
        return lax.rem(z + i, NZ)

    def ring_device(col, step):
        pos = [x, y, z]
        axis, n = COLOURS[col][:2]
        pos[axis] = lax.rem(pos[axis] + step + n, n)
        return device_of(*pos, c)

    barrier = pltpu.get_barrier_semaphore()

    def greet(device):
        pl.semaphore_signal(barrier, inc=1, device_id=device, device_id_type=MESH)

    greet(partner)
    for i in range(1, NX):
        greet(device_of(x_peer(i), y, z, c))
    for i in range(1, NY):
        greet(device_of(x, y_peer(i), z, c))
        greet((u, y_peer(i) * 2 + 1 - x_hi))
    for i in range(1, NZ):
        greet(device_of(x, y, z_peer(i), c))
    pl.semaphore_wait(barrier, 17)

    pieces = (w_in.at[:, pl.ds(0, 384)], w_in.at[:, pl.ds(384, 128)], w_out)
    slots = (
        gz.at[c, mine, z, y * 2 + x_lo],
        gx.at[c, mine, x, (y // 2) * NZ + z],
        gy.at[c, mine, y, x_lo * NZ + z],
    )
    own = [pltpu.make_async_copy(pieces[k], slots[k], loc.at[k]) for k in range(3)]
    own.append(pltpu.make_async_copy(tab, tabs.at[c, x_lo, z], loc.at[3]))
    for copy in own:
        copy.start()
    for i in range(1, NZ):
        device = device_of(x, y, z_peer(i), c)
        for col in (1, 2):
            remote(pieces[col], slots[col], st1_send.at[col], st1_recv.at[col], device).start()
    for i in range(1, NX):
        remote(pieces[0], slots[0], st1_send.at[0], st1_recv.at[0], device_of(x_peer(i), y, z, c)).start()
    for i in range(1, NZ):
        remote(tab, tabs.at[c, x_lo, z], tab_send.at[0], tab_recv.at[0], device_of(x, y, z_peer(i), c)).start()
    for copy in own:
        copy.wait()

    line_x = gx.at[c, mine, x, pl.ds((y // 2) * NZ, NZ)]
    line_y = gy.at[c, mine, y, pl.ds(x_lo * NZ, NZ)]
    wait_bytes(gx.at[c, mine, x, pl.ds(0, NZ - 1)], st1_recv.at[1])
    for i in range(1, NY):
        remote(line_x, line_x, st2_send.at[1], x2_recv.at[y], device_of(x, y_peer(i), z, c)).start()
    wait_bytes(gy.at[c, mine, y, pl.ds(0, NZ - 1)], st1_recv.at[2])
    for i in range(1, NX):
        remote(line_y, line_y, st2_send.at[2], y2_recv.at[x], device_of(x_peer(i), y, z, c)).start()
    wait_bytes(gz.at[c, 0, z, pl.ds(0, NX - 1)], st1_recv.at[0])
    for g in range(2):
        line_z = gz.at[c, g, z, pl.ds(y * 2, 2)]
        for i in range(1, NY):
            remote(line_z, line_z, z2_send.at[g], z2_recv.at[g], device_of(x, y_peer(i), z, c)).start()

    for k, (src, dst) in enumerate(((ev, xr), (ct, dr))):
        pltpu.make_async_copy(src.at[pl.ds(t * HIST, HIST)], dst.at[t], loc.at[4 + k]).start()
        for i in range(1, HEADS):
            q = lax.rem(t + i, HEADS)
            remote(src.at[pl.ds(q * HIST, HIST)], dst.at[t], a2a_send.at[k], a2a_recv.at[k], (u, q)).start()

    wait_bytes(tabs.at[c, x_lo, pl.ds(0, NZ - 1)], tab_recv.at[0])
    rows_tab = tabs.at[c, x_lo]
    remote(rows_tab, rows_tab, tab_send.at[1], tab_recv.at[1], device_of(x + 1 - 2 * x_lo, y, z, c)).start()

    def half_of(ref, half, m):
        return ref.at[pl.ds(half * (m // 2), m // 2)]

    def ring_sem(g, col, k, direction, half):
        return g * 32 + BASE[col] + (direction * (COLOURS[col][1] // 2) + k) * 2 + half

    def block(col, g, idx, half):
        return half_of(gs[col].at[c, g, idx], half, COLOURS[col][2])

    def forward(col, g, idx, half):
        part = block(col, g, idx, half)
        remote(part, part, fw_send.at[g * 3 + col], fw_recv.at[g * 3 + col], partner).start()

    def ag_send_part(col, g, k, direction, half):
        n = COLOURS[col][1]
        step = 1 - 2 * direction
        part = block(col, g, lax.rem(place[col] - step * k + n, n), half)
        s = ring_sem(g, col, k, direction, half)
        remote(part, part, ag_send.at[s], ag_recv.at[s], ring_device(col, step)).start()

    def ag_start(g):
        for col in ORDER:
            m = COLOURS[col][2]
            if col == 0:
                wait_bytes(gz.at[c, g, z, pl.ds(0, 6)], z2_recv.at[g])
            elif col == 1:
                for yy in range(2):
                    src = yy * 2 + lax.rem(g + x_hi, 2)
                    pl.when(src != y)(lambda: wait_bytes(gx.at[c, g, x, pl.ds(yy * NZ, NZ)], x2_recv.at[src]))
            else:
                for xl in range(2):
                    src = lax.rem(g + y, 2) * 2 + xl
                    pl.when(src != x)(lambda: wait_bytes(gy.at[c, g, y, pl.ds(xl * NZ, NZ)], y2_recv.at[src]))
            for half in (0, 1):
                for direction in (0, 1):
                    ag_send_part(col, g, 0, direction, half)
            for half in (0, 1):
                forward(col, g, place[col], half)

    def ag_step(g, k):
        for col in ORDER:
            n = COLOURS[col][1]
            last = n // 2 - 1

            def part_step(half, direction):
                step = 1 - 2 * direction
                idx = lax.rem(place[col] - step * (k + 1) + n, n)
                wait_bytes(block(col, g, idx, half), ag_recv.at[ring_sem(g, col, k, direction, half)])
                forward(col, g, idx, half)
                more = k + 1 <= last if half == direction else k + 1 < last
                when(more, lambda: ag_send_part(col, g, k + 1, direction, half))

            for half in (0, 1):
                for direction in (0, 1):
                    active = k <= last if half == direction else k < last
                    when(active, lambda: part_step(half, direction))

    def ag_done(g):
        for col in range(3):
            wait_bytes(gs[col].at[1 - c, g], fw_recv.at[g * 3 + col])

    def norm_rows():
        pltpu.make_async_copy(xr.at[t], xr.at[t], loc.at[4]).wait()
        wait_bytes(xr.at[pl.ds(0, HEADS - 1)], a2a_recv.at[0])
        for i in range(HIST):
            rows = pl.ds(i * SEQ, SEQ)
            xs = jnp.concatenate([xr[k, i] for k in range(HEADS)], axis=1).astype(F32)
            cen = xs - jnp.mean(xs, axis=1, keepdims=True)
            rstd = lax.rsqrt(jnp.mean(cen * cen, axis=1, keepdims=True) + EPS)
            nfi = cen * rstd
            nf[rows, :] = nfi
            rstd_s[rows, :] = jnp.broadcast_to(rstd, (SEQ, 128))
            nbi = nfi.astype(BF16)
            nb[rows, :] = nbi
            nbt[:, rows] = nbi.T

    def mask_rows():
        pltpu.make_async_copy(dr.at[t], dr.at[t], loc.at[5]).wait()
        wait_bytes(dr.at[pl.ds(0, HEADS - 1)], a2a_recv.at[1])
        wait_bytes(tabs.at[1 - c], tab_recv.at[2])
        lens = jnp.zeros((1, 128), F32)
        for cc in range(2):
            for xl in range(2):
                rows = tabs[cc, xl]
                lens = lens + jnp.sum(
                    jnp.where(rows[:, 0, :] == u, rows[:, 1, :], 0).astype(F32), axis=0, keepdims=True
                )
        lane = lax.broadcasted_iota(jnp.int32, (1, 128), 1)
        pos = lax.broadcasted_iota(jnp.int32, (SEQ, D), 0).astype(F32)
        for i in range(HIST):
            rows = pl.ds(i * SEQ, SEQ)
            length = jnp.sum(jnp.where(lane == t * HIST + i, lens, 0.0), axis=1, keepdims=True)
            di = jnp.concatenate([dr[k, i] for k in range(HEADS)], axis=1).astype(F32)
            di = jnp.where(pos < length, di, 0.0).astype(BF16)
            dm[rows, :] = di
            dmt[:, rows] = di.T
        dn[...] = jnp.zeros_like(dn)

    def head(g, hy):
        hx = lax.rem(g + hy, 2)
        for xl in range(2):
            for zz in range(NZ):
                for cc in range(2):
                    r = pl.ds(((xl * NZ + zz) * 2 + cc) * 32, 32)
                    wh[r, pl.ds(0, 384)] = gz[cc, g, zz, hy * 2 + xl]
                    wh[r, pl.ds(384, 128)] = gx[cc, g, hx * 2 + xl, (hy // 2) * NZ + zz]
                    wo[r, :] = gy[cc, g, hy, xl * NZ + zz]
        scale = HD ** (-0.5)
        zv = dot(nb[...], wh[...], NN)
        gv, sg = silu_parts(zv)
        gv = gv.astype(BF16)
        grad_h = dot(dm[...], wo[...], NN)
        uf = gv[:, 0:128].astype(F32)
        vp, qp, kp = gv[:, 128:256], gv[:, 256:384], gv[:, 384:512]
        hs = [slice(i * SEQ, i * SEQ + SEQ) for i in range(HIST)]

        def each(f):
            return jnp.concatenate([f(r) for r in hs], axis=0)

        s = each(lambda r: dot(qp[r], kp[r], NT)) * scale
        causal = lax.broadcasted_iota(jnp.int32, (SEQ, SEQ), 1) <= lax.broadcasted_iota(jnp.int32, (SEQ, SEQ), 0)
        causal = jnp.concatenate([causal] * HIST, axis=0)
        ss, sgs = silu_parts(s)
        at = jnp.where(causal, ss / SEQ, 0.0).astype(BF16)
        yv = each(lambda r: dot(at[r], vp[r], NN))
        ycen = yv - jnp.mean(yv, axis=1, keepdims=True)
        yrstd = lax.rsqrt(jnp.mean(ycen * ycen, axis=1, keepdims=True) + EPS)
        yn = ycen * yrstd
        hb_s[...] = (yn * uf).astype(BF16)
        dz_s[:, 0:128] = (grad_h * yn * sg[:, 0:128]).astype(BF16)
        gyn = grad_h * uf
        dy = (
            (gyn - jnp.mean(gyn, axis=1, keepdims=True) - yn * jnp.mean(gyn * yn, axis=1, keepdims=True)) * yrstd
        ).astype(BF16)
        da = each(lambda r: dot(dy[r], vp[r], NT))
        dz_s[:, 128:256] = (each(lambda r: dot(at[r], dy[r], TN)) * sg[:, 128:256]).astype(BF16)
        ds_ = jnp.where(causal, da * sgs * (scale / SEQ), 0.0).astype(BF16)
        dz_s[:, 256:384] = (each(lambda r: dot(ds_[r], kp[r], NN)) * sg[:, 256:384]).astype(BF16)
        dz_s[:, 384:512] = (each(lambda r: dot(ds_[r], qp[r], TN)) * sg[:, 384:512]).astype(BF16)
        for j in range(4):
            gw = dot(nbt[pl.ds(j * 256, 256), :], dz_s[...], NN).astype(BF16)
            go = dot(dmt[pl.ds(j * 256, 256), :], hb_s[...], NN).astype(BF16)
            for k in range(8):
                uu = j * 8 + k
                cc, zz, xl = uu % 2, (uu // 2) % NZ, uu // (2 * NZ)
                pz[cc, g, zz, hy * 2 + xl] = gw[k * 32 : k * 32 + 32, 0:384]
                px[cc, g, hx * 2 + xl, (hy // 2) * NZ + zz] = gw[k * 32 : k * 32 + 32, 384:512]
                py[cc, g, hy, xl * NZ + zz] = go[k * 32 : k * 32 + 32, :]
            dn[:, pl.ds(j * 256, 256)] += dot(dz_s[...], wh[pl.ds(j * 256, 256), :], NT)

    def rows_out():
        for i in range(HIST):
            rows = pl.ds(i * SEQ, SEQ)
            dni, nfi = dn[rows, :], nf[rows, :]
            branch = (
                dni - jnp.mean(dni, axis=1, keepdims=True) - nfi * jnp.mean(dni * nfi, axis=1, keepdims=True)
            ) * rstd_s[rows, 0:1]
            out = (dm[rows, :].astype(F32) + branch).astype(BF16)
            for k in range(HEADS):
                dr[k, i] = out[:, k * 128 : k * 128 + 128]

    def index(col, off):
        n = COLOURS[col][1]
        return lax.rem(place[col] + off + n, n)

    def par_sem(g, col, off, half):
        n = COLOURS[col][1]
        return g * 32 + BASE[col] + lax.rem(off + n, n) * 2 + half

    def rs_start(g):
        for j in range(NZ // 2 + 1):
            for col in ORDER:
                n, m = COLOURS[col][1:3]
                if j > n // 2:
                    continue
                for off in sorted({(n // 2 - j) % n, (j - n // 2) % n}):
                    for half in (0, 1):
                        s = par_sem(g, col, off, half)
                        remote(
                            half_of(ps[col].at[1 - c, g, index(col, off)], half, m),
                            half_of(ts[col].at[g, index(col, off)], half, m),
                            par_send.at[s], par_recv.at[s], partner,
                        ).start()

    def rs_add(g, col, off, half, from_ring):
        m = COLOURS[col][2]
        own_part = half_of(ps[col].at[c, g, index(col, off)], half, m)
        other = half_of(ts[col].at[g, index(col, off)], half, m)
        wait_bytes(other, par_recv.at[par_sem(g, col, off, half)])
        got = []
        for k, direction in from_ring:
            s = ring_sem(g, col, k, direction, half)
            wait_bytes(rings[col].at[s - BASE[col] - g * 32 + g * 2 * COLOURS[col][1]], rs_recv.at[s])
            got.append(rings[col].at[s - BASE[col] - g * 32 + g * 2 * COLOURS[col][1]])

        @pl.loop(0, m // 2)
        def _(i):
            v = own_part[i].astype(F32) + other[i].astype(F32)
            for ref in got:
                v = v + ref[i].astype(F32)
            own_part[i] = v.astype(BF16)

    def rs_step(g, k):
        for col in ORDER:
            n, m = COLOURS[col][1:3]
            top = n // 2

            def part_step(half, direction, from_ring):
                off = top - k if direction == 0 else k - top
                rs_add(g, col, off, half, ((k - 1, direction),) if from_ring else ())
                s = ring_sem(g, col, k, direction, half)
                remote(
                    half_of(ps[col].at[c, g, index(col, off)], half, m),
                    rings[col].at[s - BASE[col] - g * 32 + g * 2 * n],
                    rs_send.at[s], rs_recv.at[s], ring_device(col, 1 - 2 * direction),
                ).start()

            for half in (0, 1):
                for direction in (0, 1):
                    first = 0 if half == direction else 1
                    when(k == first, lambda: part_step(half, direction, False))
                    if isinstance(k, int):
                        when(first < k < top, lambda: part_step(half, direction, True))
                    elif first + 1 < top:
                        pl.when((k > first) & (k < top))(lambda: part_step(half, direction, True))

    def rs_lines(g):
        for col in ORDER:
            n = COLOURS[col][1]
            for half in (0, 1):
                rs_add(g, col, 0, half, tuple((n // 2 - 1, d) for d in (0, 1)))
        for i in range(1, NY):
            q = y_peer(i)
            device = device_of(x, q, z, c)

            @pl.when(lax.rem(q + x_hi, 2) == g)
            def _():
                remote(
                    px.at[c, g, x, pl.ds((q // 2) * NZ, NZ)], s1x.at[y], o1_send.at[0], o1_recv.at[0], device
                ).start()

        for i in range(1, NX):
            q = x_peer(i)
            device = device_of(q, y, z, c)

            @pl.when(lax.rem(y + q // 2, 2) == g)
            def _():
                remote(
                    py.at[c, g, y, pl.ds(lax.rem(q, 2) * NZ, NZ)], s1y.at[x], o1_send.at[1], o1_recv.at[1], device
                ).start()

        for i in range(1, NY):
            q = y_peer(i)
            remote(
                pz.at[c, g, z, pl.ds(q * 2, 2)], s1z.at[g, y], o1z_send.at[g], o1z_recv.at[g],
                device_of(x, q, z, c),
            ).start()

    def sum_into(own_part, parts, count):
        @pl.loop(0, count)
        def _(i):
            v = own_part[i].astype(F32)
            for ref in parts:
                v = v + ref[i].astype(F32)
            own_part[i] = v.astype(BF16)

    ag_start(0)
    ag_step(0, 0)
    wait_bytes(tabs.at[c, 1 - x_lo], tab_recv.at[1])
    remote(tabs.at[c], tabs.at[c], tab_send.at[2], tab_recv.at[2], partner).start()
    ag_step(0, 1)
    ag_step(0, 2)
    ag_start(1)
    norm_rows()
    ag_step(0, 3)
    mask_rows()
    ag_done(0)

    @pl.loop(0, NY)
    def _(j):
        head(0, j)
        ag_step(1, j)

    rs_start(0)
    ag_done(1)

    @pl.loop(0, NY)
    def _(j):
        head(1, j)
        rs_step(0, j)

    rs_start(1)
    rows_out()
    for i in range(1, HEADS):
        q = lax.rem(t + i, HEADS)
        remote(dr.at[q], grad_x.at[pl.ds(t * HIST, HIST)], out_send, out_recv, (u, q)).start()
    pltpu.make_async_copy(dr.at[t], grad_x.at[pl.ds(t * HIST, HIST)], loc.at[6]).start()
    rs_lines(0)
    for k in range(NZ // 2):
        rs_step(1, k)
    rs_lines(1)

    wait_bytes(s1x.at[pl.ds(0, NY - 1)], o1_recv.at[0])
    line_px = px.at[c, mine, x, pl.ds((y // 2) * NZ, NZ)]
    sum_into(line_px, [s1x.at[y_peer(i)] for i in range(1, NY)], NZ)
    for i in range(1, NZ):
        q = z_peer(i)
        remote(line_px.at[q], s2x.at[z], o2_send.at[1], o2_recv.at[1], device_of(x, y, q, c)).start()
    wait_bytes(s1y.at[pl.ds(0, NX - 1)], o1_recv.at[1])
    line_py = py.at[c, mine, y, pl.ds(x_lo * NZ, NZ)]
    sum_into(line_py, [s1y.at[x_peer(i)] for i in range(1, NX)], NZ)
    for i in range(1, NZ):
        q = z_peer(i)
        remote(line_py.at[q], s2y.at[z], o2_send.at[2], o2_recv.at[2], device_of(x, y, q, c)).start()
    for g in range(2):
        wait_bytes(s1z.at[g, pl.ds(0, NY - 1)], o1z_recv.at[g])
        sum_into(pz.at[c, g, z, pl.ds(y * 2, 2)], [s1z.at[g, y_peer(i)] for i in range(1, NY)], 2)
    for i in range(1, NX):
        q = x_peer(i)
        remote(
            pz.at[c, lax.rem(y + q // 2, 2), z, y * 2 + lax.rem(q, 2)], s2z.at[x], o2_send.at[0], o2_recv.at[0],
            device_of(q, y, z, c),
        ).start()

    wait_bytes(s2x.at[pl.ds(0, NZ - 1)], o2_recv.at[1])
    total = line_px[z].astype(F32)
    for i in range(1, NZ):
        total = total + s2x[z_peer(i)].astype(F32)
    grad_wi[:, pl.ds(384, 128)] = total
    wait_bytes(s2y.at[pl.ds(0, NZ - 1)], o2_recv.at[2])
    total = line_py[z].astype(F32)
    for i in range(1, NZ):
        total = total + s2y[z_peer(i)].astype(F32)
    grad_wo[...] = total
    wait_bytes(s2z.at[pl.ds(0, NX - 1)], o2_recv.at[0])
    total = pz[c, mine, z, y * 2 + x_lo].astype(F32)
    for i in range(1, NX):
        total = total + s2z[x_peer(i)].astype(F32)
    grad_wi[:, pl.ds(0, 384)] = total

    wait_bytes(gx.at[c, mine, x, pl.ds(0, NZ - 1)], st1_send.at[1])
    wait_bytes(gy.at[c, mine, y, pl.ds(0, NZ - 1)], st1_send.at[2])
    wait_bytes(gz.at[c, 0, z, pl.ds(0, NX - 1)], st1_send.at[0])
    wait_bytes(s1x.at[pl.ds(0, NY - 1)], st2_send.at[1])
    wait_bytes(s1y.at[pl.ds(0, NX - 1)], st2_send.at[2])
    for g in range(2):
        wait_bytes(gz.at[c, g, z, pl.ds(0, 6)], z2_send.at[g])
        wait_bytes(s1z.at[g, pl.ds(0, NY - 1)], o1z_send.at[g])
    wait_bytes(tabs.at[c, x_lo, pl.ds(0, NZ - 1)], tab_send.at[0])
    wait_bytes(tabs.at[c, x_lo], tab_send.at[1])
    wait_bytes(tabs.at[c], tab_send.at[2])
    wait_bytes(s1x.at[pl.ds(0, NY - 1)], o1_send.at[0])
    wait_bytes(s1y.at[pl.ds(0, NX - 1)], o1_send.at[1])
    wait_bytes(s2z.at[pl.ds(0, NX - 1)], o2_send.at[0])
    wait_bytes(s2x.at[pl.ds(0, NZ - 1)], o2_send.at[1])
    wait_bytes(s2y.at[pl.ds(0, NZ - 1)], o2_send.at[2])
    for k, ref in enumerate((xr, dr)):
        wait_bytes(ref.at[pl.ds(0, HEADS - 1)], a2a_send.at[k])
    for g in range(2):
        for col in range(3):
            n, m = COLOURS[col][1:3]
            wait_bytes(gs[col].at[c, g], fw_send.at[g * 3 + col])
            for half in (0, 1):
                for direction in (0, 1):
                    for k in range(n // 2):
                        s = ring_sem(g, col, k, direction, half)
                        part = half_of(gs[col].at[c, g, 0], half, m)
                        if half == direction or k < n // 2 - 1:
                            wait_bytes(part, ag_send.at[s])
                        if half == direction or k > 0:
                            wait_bytes(part, rs_send.at[s])
                for off in range(n):
                    wait_bytes(half_of(ts[col].at[g, 0], half, m), par_send.at[par_sem(g, col, off, half)])
    pltpu.make_async_copy(dr.at[t], grad_x.at[pl.ds(t * HIST, HIST)], loc.at[6]).wait()
    wait_bytes(dr.at[pl.ds(0, HEADS - 1)], out_send)
    wait_bytes(dr.at[pl.ds(0, HEADS - 1)], out_recv)


def local(events, cotangent, w_in, w_out, slot_source, slot_length):
    tab = jnp.pad(jnp.stack([slot_source, slot_length]), ((0, 6), (0, 96)))
    any_ = pl.BlockSpec(memory_space=pl.ANY)
    vmem = pl.BlockSpec(memory_space=pltpu.VMEM)
    shape = jax.ShapeDtypeStruct
    dma = pltpu.SemaphoreType.DMA
    both = [pltpu.VMEM((2, 2, n, m, 32, w), BF16) for _, n, m, w in COLOURS]
    theirs = [pltpu.VMEM((2, n, m, 32, w), BF16) for _, n, m, w in COLOURS]
    rings = [pltpu.VMEM((4 * n, m // 2, 32, w), BF16) for _, n, m, w in COLOURS]
    lines = [
        pltpu.VMEM((2, NY, 2, 32, 384), BF16),
        pltpu.VMEM((NY, NZ, 32, 128), BF16),
        pltpu.VMEM((NX, NZ, 32, 128), BF16),
        pltpu.VMEM((NX, 32, 384), BF16),
        pltpu.VMEM((NZ, 32, 128), BF16),
        pltpu.VMEM((NZ, 32, 128), BF16),
    ]
    work = [
        pltpu.VMEM((HEADS, HIST, SEQ, 128), BF16),
        pltpu.VMEM((HEADS, HIST, SEQ, 128), BF16),
        pltpu.VMEM((2, 2, NZ, 8, 128), jnp.int32),
        pltpu.VMEM((ROWS, D), F32),
        pltpu.VMEM((ROWS, D), BF16),
        pltpu.VMEM((D, ROWS), BF16),
        pltpu.VMEM((ROWS, D), BF16),
        pltpu.VMEM((D, ROWS), BF16),
        pltpu.VMEM((ROWS, 128), F32),
        pltpu.VMEM((ROWS, D), F32),
        pltpu.VMEM((D, 512), BF16),
        pltpu.VMEM((D, 128), BF16),
        pltpu.VMEM((ROWS, 512), BF16),
        pltpu.VMEM((ROWS, 128), BF16),
    ]
    sems = [
        dma((7,)), dma((3,)), dma((3,)), dma((3,)), dma((2,)), dma((2,)), dma((NY,)), dma((NX,)),
        dma((64,)), dma((64,)), dma((6,)), dma((6,)), dma((2,)), dma((2,)), dma((3,)), dma((3,)),
        dma((64,)), dma((64,)), dma((64,)), dma((64,)),
        dma((2,)), dma((2,)), dma((2,)), dma((2,)), dma((3,)), dma((3,)), dma, dma,
    ]
    return pl.pallas_call(
        kernel,
        out_shape=(shape((32, SEQ, 128), BF16), shape((32, 512), F32), shape((32, 128), F32)),
        in_specs=[any_, any_, vmem, vmem, vmem],
        out_specs=(any_, vmem, vmem),
        scratch_shapes=both + both + theirs + rings + lines + work + sems,
        compiler_params=pltpu.CompilerParams(
            has_side_effects=True, collective_id=0, vmem_limit_bytes=64 * 1024 * 1024 - 131072
        ),
        name="step",
    )(events, cotangent, w_in, w_out, tab)


def solution(mesh):
    in_specs = (
        P("user", None, "tensor"),
        P("user", None, "tensor"),
        P("user", "tensor"),
        P("user", "tensor"),
        P("user"),
        P("user"),
    )
    out_specs = (P("user", None, "tensor"), P("user", "tensor"), P("user", "tensor"))
    return jax.shard_map(local, mesh=mesh, in_specs=in_specs, out_specs=out_specs, check_vma=False)
```

time: 968 us -> 164 us (0.17)
  waiting for transfers between devices: 735 us -> 0 us
  Pallas kernels: 0 us -> 158 us
  matrix products: 60.4 us -> 0 us
  blocking collectives: 55.6 us -> 0 us
  local copies, waits for them, and re-layouts: 54.9 us -> 4.92 us
  other arithmetic: 24.9 us -> 0.01 us
  starting transfers between devices: 16.1 us -> 0 us
  between operations: 16.3 us -> 0.67 us
    psum x1 -> x0, waiting for transfers between devices: 334 us -> none  [local(): dn_all = lax.psum(dn, 'tensor')]
    reduce_scatter x2 -> x0, waiting for transfers between devices: 201 us -> none  [the longest x1 116 us: local(): lax.psum_scatter(lax.dot_general(columns, dz, (((0,), (0,)), ((), ())), p...]
    pallas_call x0 -> x1, Pallas kernels: none -> 158 us  [local(): pl.pallas_call(kernel, out_shape=(shape((32, SEQ, 128), BF16), shape((32,...]
    all_gather x3 -> x0, waiting for transfers between devices: 154 us -> none  [the longest x1 59.8 us: local(): w_in_cols = lax.all_gather(w_in, 'user', axis=0, tiled=True)]
    dot_general x29 -> x0, matrix products: 60.4 us -> none  [the longest x4 12.3 us: local(): jnp.einsum('hqe,hke->hqk', grad_y, vpart, preferred_element_type=jnp.floa...]
    all_to_all x3 -> x0, waiting for transfers between devices: 44 us -> none  [the longest x1 22.5 us: local(): lax.all_to_all(send_d, 'user', split_axis=0, concat_axis=0, tiled=True)]
    all_gather x1 -> x0, blocking collectives: 36.2 us -> none  [local(): w_out_cols = lax.all_gather(w_out, 'user', axis=0, tiled=True)]
    gather x4 -> x0, local copies, waits for them, and re-layouts: 25.2 us -> none  [the longest x1 12.1 us: local(): jnp.take(dxp, rows_at.reshape(-1), axis=0)]
  transfers between devices with their start and end apart: 9 -> 0, of which waited for: 8 -> 0; matrix products, arithmetic and copies ran while one was open for 8% -> 0% of each run, Pallas kernels for 0% -> 0%
where the time goes in v2:
time: 164 us; the launch traced here: 163 us
  Pallas kernels  158 us (96%)
  local copies, waits for them, and re-layouts  4.92 us (3%)
    pallas_call x1, Pallas kernels, local(): pl.pallas_call(kernel, out_shape=(shape((32, SEQ, 128), BF16), shape((32,...  158 us
    unnamed x11, local copies, waits for them, and re-layouts  4.32 us

profile of v2, /device:TPU:8, one launch (start us, length us, event | category | flops | bytes accessed | tf_op | source)
XLA Modules:
  0.0 163.2 jit_solution(9217820635793429182)
XLA Ops:
  0.6 0.0 copy-start.2
  0.6 0.0 copy-start.3
  0.7 0.6 copy-done.2
  1.3 0.0 copy-done.3
  1.3 0.6 pad.4.tab
  1.9 157.6 %step.1 = (bf16[32,128,128]{2,1,0:T(8,128)(2,1)}, f32[32,512]{1,0:T(8,128)}, f32[32,128]{1,0:T(8,128)}) custom-call(bf16[32,128,128]{2,1,0:T(8,128)(2,1)} %ev.1, bf16[32,128,128]{2,1,0:T(8,128)(2,1)} %ct.1, bf16[32,512]{1,0:T(8,128)(2,1)} %w_in.1, bf16[32,128]{1,0:T(8,128)(2,1)} %w_out.1, s32[8,128]{1,0:T(8,128)} %pad.4.tab), custom_call_target="tpu_custom_call" | custom-call | tf_op jit(solution)/shard_map/step/pallas_call | solution.py:572
  159.5 0.0 copy-start
  159.5 2.3 %copy.12 = bf16[32,128,128]{2,1,0:T(8,128)(2,1)} copy(bf16[32,128,128]{2,1,0:T(8,128)(2,1)} %get-tuple-element.6) | data formatting | bytes 2097152
  161.9 0.0 copy-done
  161.9 0.0 copy-start.1
  161.9 0.6 copy.13
  162.5 0.1 copy-done.1
  162.6 0.6 copy.14
  (1 shorter events, 0.0 us)
Async XLA Ops:
  0.6 0.7 copy-start.2
  0.6 0.7 copy-start.3
  159.5 2.4 %copy-start = (f32[32,512]{1,0:T(8,128)S(1)}, f32[32,512]{1,0:T(8,128)}, u32[]{:S(2)}) copy-start(f32[32,512]{1,0:T(8,128)} %get-tuple-element.7) | copy-start | bytes 196612
  161.9 0.7 copy-start.1

commit v3 on v2

--- a/solution.py
+++ b/solution.py
@@ -18,8 +18,7 @@
 D = 1024
 
 COLOURS = ((2, NZ, 8, 384), (0, NX, 16, 128), (1, NY, 16, 128))
-ORDER = (1, 2, 0)
-BASE = (0, 16, 24)
+ZM = 8
 
 
 def device_of(x, y, z, c):
@@ -62,6 +61,7 @@
     xr, dr, tabs, nf, nb, nbt, dm, dmt, rstd_s, dn, wh, wo, dz_s, hb_s,
     loc, st1_send, st1_recv, st2_send, z2_send, z2_recv, x2_recv, y2_recv, ag_send, ag_recv, fw_send, fw_recv,
     a2a_send, a2a_recv, tab_send, tab_recv, par_send, par_recv, rs_send, rs_recv,
+    last_send, last_recv, rl_send, rl_recv,
     o1_send, o1z_send, o1_recv, o1z_recv, o2_send, o2_recv, out_send, out_recv,
 ):
     u = lax.axis_index("user")
@@ -86,11 +86,12 @@
     def z_peer(i):
         return lax.rem(z + i, NZ)
 
-    def ring_device(col, step):
-        pos = [x, y, z]
-        axis, n = COLOURS[col][:2]
-        pos[axis] = lax.rem(pos[axis] + step + n, n)
-        return device_of(*pos, c)
+    def z_device(step):
+        return device_of(x, y, lax.rem(z + step + NZ, NZ), c)
+
+    def last_peer(col, i):
+        q = x_peer(i) if col == 1 else y_peer(i)
+        return q, device_of(q, y, z, c) if col == 1 else device_of(x, q, z, c)
 
     barrier = pltpu.get_barrier_semaphore()
 
@@ -117,17 +118,24 @@
     own.append(pltpu.make_async_copy(tab, tabs.at[c, x_lo, z], loc.at[3]))
     for copy in own:
         copy.start()
+    for i in range(1, NX):
+        remote(pieces[0], slots[0], st1_send.at[0], st1_recv.at[0], device_of(x_peer(i), y, z, c)).start()
     for i in range(1, NZ):
         device = device_of(x, y, z_peer(i), c)
         for col in (1, 2):
             remote(pieces[col], slots[col], st1_send.at[col], st1_recv.at[col], device).start()
-    for i in range(1, NX):
-        remote(pieces[0], slots[0], st1_send.at[0], st1_recv.at[0], device_of(x_peer(i), y, z, c)).start()
     for i in range(1, NZ):
         remote(tab, tabs.at[c, x_lo, z], tab_send.at[0], tab_recv.at[0], device_of(x, y, z_peer(i), c)).start()
     for copy in own:
         copy.wait()
 
+    def line_z(g):
+        line = gz.at[c, g, z, pl.ds(y * 2, 2)]
+        for i in range(1, NY):
+            remote(line, line, z2_send.at[g], z2_recv.at[g], device_of(x, y_peer(i), z, c)).start()
+
+    wait_bytes(gz.at[c, 0, z, pl.ds(0, NX - 1)], st1_recv.at[0])
+    line_z(0)
     line_x = gx.at[c, mine, x, pl.ds((y // 2) * NZ, NZ)]
     line_y = gy.at[c, mine, y, pl.ds(x_lo * NZ, NZ)]
     wait_bytes(gx.at[c, mine, x, pl.ds(0, NZ - 1)], st1_recv.at[1])
@@ -136,78 +144,84 @@
     wait_bytes(gy.at[c, mine, y, pl.ds(0, NZ - 1)], st1_recv.at[2])
     for i in range(1, NX):
         remote(line_y, line_y, st2_send.at[2], y2_recv.at[x], device_of(x_peer(i), y, z, c)).start()
-    wait_bytes(gz.at[c, 0, z, pl.ds(0, NX - 1)], st1_recv.at[0])
-    for g in range(2):
-        line_z = gz.at[c, g, z, pl.ds(y * 2, 2)]
-        for i in range(1, NY):
-            remote(line_z, line_z, z2_send.at[g], z2_recv.at[g], device_of(x, y_peer(i), z, c)).start()
-
-    for k, (src, dst) in enumerate(((ev, xr), (ct, dr))):
-        pltpu.make_async_copy(src.at[pl.ds(t * HIST, HIST)], dst.at[t], loc.at[4 + k]).start()
-        for i in range(1, HEADS):
-            q = lax.rem(t + i, HEADS)
-            remote(src.at[pl.ds(q * HIST, HIST)], dst.at[t], a2a_send.at[k], a2a_recv.at[k], (u, q)).start()
+    line_z(1)
+
+    def send_rows():
+        for k, (src, dst) in enumerate(((ev, xr), (ct, dr))):
+            pltpu.make_async_copy(src.at[pl.ds(t * HIST, HIST)], dst.at[t], loc.at[4 + k]).start()
+            for i in range(1, HEADS):
+                q = lax.rem(t + i, HEADS)
+                remote(src.at[pl.ds(q * HIST, HIST)], dst.at[t], a2a_send.at[k], a2a_recv.at[k], (u, q)).start()
 
     wait_bytes(tabs.at[c, x_lo, pl.ds(0, NZ - 1)], tab_recv.at[0])
     rows_tab = tabs.at[c, x_lo]
     remote(rows_tab, rows_tab, tab_send.at[1], tab_recv.at[1], device_of(x + 1 - 2 * x_lo, y, z, c)).start()
 
-    def half_of(ref, half, m):
-        return ref.at[pl.ds(half * (m // 2), m // 2)]
-
-    def ring_sem(g, col, k, direction, half):
-        return g * 32 + BASE[col] + (direction * (COLOURS[col][1] // 2) + k) * 2 + half
-
-    def block(col, g, idx, half):
-        return half_of(gs[col].at[c, g, idx], half, COLOURS[col][2])
-
-    def forward(col, g, idx, half):
-        part = block(col, g, idx, half)
+    def half_of(ref, half):
+        return ref.at[pl.ds(half * (ZM // 2), ZM // 2)]
+
+    def ring_sem(g, k, direction, half):
+        return g * 16 + (direction * (NZ // 2) + k) * 2 + half
+
+    def block(g, idx, half):
+        return half_of(gz.at[c, g, idx], half)
+
+    def forward(col, g, part):
         remote(part, part, fw_send.at[g * 3 + col], fw_recv.at[g * 3 + col], partner).start()
 
-    def ag_send_part(col, g, k, direction, half):
-        n = COLOURS[col][1]
+    def ring_part(g, k, direction, half):
         step = 1 - 2 * direction
-        part = block(col, g, lax.rem(place[col] - step * k + n, n), half)
-        s = ring_sem(g, col, k, direction, half)
-        remote(part, part, ag_send.at[s], ag_recv.at[s], ring_device(col, step)).start()
-
-    def ag_start(g):
-        for col in ORDER:
-            m = COLOURS[col][2]
-            if col == 0:
-                wait_bytes(gz.at[c, g, z, pl.ds(0, 6)], z2_recv.at[g])
-            elif col == 1:
-                for yy in range(2):
-                    src = yy * 2 + lax.rem(g + x_hi, 2)
-                    pl.when(src != y)(lambda: wait_bytes(gx.at[c, g, x, pl.ds(yy * NZ, NZ)], x2_recv.at[src]))
-            else:
-                for xl in range(2):
-                    src = lax.rem(g + y, 2) * 2 + xl
-                    pl.when(src != x)(lambda: wait_bytes(gy.at[c, g, y, pl.ds(xl * NZ, NZ)], y2_recv.at[src]))
-            for half in (0, 1):
-                for direction in (0, 1):
-                    ag_send_part(col, g, 0, direction, half)
-            for half in (0, 1):
-                forward(col, g, place[col], half)
+        part = block(g, lax.rem(z - step * k + NZ, NZ), half)
+        s = ring_sem(g, k, direction, half)
+        remote(part, part, ag_send.at[s], ag_recv.at[s], z_device(step)).start()
+
+    def last_sem(g, col, q):
+        return (g * 2 + col - 1) * 4 + q
+
+    def ag_start_z(g):
+        wait_bytes(gz.at[c, g, z, pl.ds(0, 6)], z2_recv.at[g])
+        for half in (0, 1):
+            for direction in (0, 1):
+                ring_part(g, 0, direction, half)
+        forward(0, g, gz.at[c, g, z])
+
+    def ag_start_xy(g):
+        for yy in range(2):
+            src = yy * 2 + lax.rem(g + x_hi, 2)
+            pl.when(src != y)(lambda: wait_bytes(gx.at[c, g, x, pl.ds(yy * NZ, NZ)], x2_recv.at[src]))
+        for xl in range(2):
+            src = lax.rem(g + y, 2) * 2 + xl
+            pl.when(src != x)(lambda: wait_bytes(gy.at[c, g, y, pl.ds(xl * NZ, NZ)], y2_recv.at[src]))
+        for col in (1, 2):
+            part = gs[col].at[c, g, place[col]]
+            for i in (1, 3, 2):
+                s = last_sem(g, col, place[col])
+                remote(part, part, last_send.at[g * 2 + col - 1], last_recv.at[s], last_peer(col, i)[1]).start()
+            forward(col, g, part)
+
+    def ag_take_xy(g):
+        for i in (1, 3, 2):
+            for col in (1, 2):
+                q = last_peer(col, i)[0]
+                part = gs[col].at[c, g, q]
+                wait_bytes(part, last_recv.at[last_sem(g, col, q)])
+                forward(col, g, part)
 
     def ag_step(g, k):
-        for col in ORDER:
-            n = COLOURS[col][1]
-            last = n // 2 - 1
-
-            def part_step(half, direction):
-                step = 1 - 2 * direction
-                idx = lax.rem(place[col] - step * (k + 1) + n, n)
-                wait_bytes(block(col, g, idx, half), ag_recv.at[ring_sem(g, col, k, direction, half)])
-                forward(col, g, idx, half)
-                more = k + 1 <= last if half == direction else k + 1 < last
-                when(more, lambda: ag_send_part(col, g, k + 1, direction, half))
-
-            for half in (0, 1):
-                for direction in (0, 1):
-                    active = k <= last if half == direction else k < last
-                    when(active, lambda: part_step(half, direction))
+        last = NZ // 2 - 1
+
+        def part_step(half, direction):
+            step = 1 - 2 * direction
+            idx = lax.rem(z - step * (k + 1) + NZ, NZ)
+            wait_bytes(block(g, idx, half), ag_recv.at[ring_sem(g, k, direction, half)])
+            more = k + 1 <= last if half == direction else k + 1 < last
+            when(more, lambda: ring_part(g, k + 1, direction, half))
+            forward(0, g, block(g, idx, half))
+
+        for half in (0, 1):
+            for direction in (0, 1):
+                active = k <= last if half == direction else k < last
+                when(active, lambda: part_step(half, direction))
 
     def ag_done(g):
         for col in range(3):
@@ -313,76 +327,87 @@
             for k in range(HEADS):
                 dr[k, i] = out[:, k * 128 : k * 128 + 128]
 
-    def index(col, off):
-        n = COLOURS[col][1]
-        return lax.rem(place[col] + off + n, n)
-
-    def par_sem(g, col, off, half):
-        n = COLOURS[col][1]
-        return g * 32 + BASE[col] + lax.rem(off + n, n) * 2 + half
-
-    def rs_start(g):
-        for j in range(NZ // 2 + 1):
-            for col in ORDER:
-                n, m = COLOURS[col][1:3]
-                if j > n // 2:
-                    continue
-                for off in sorted({(n // 2 - j) % n, (j - n // 2) % n}):
-                    for half in (0, 1):
-                        s = par_sem(g, col, off, half)
-                        remote(
-                            half_of(ps[col].at[1 - c, g, index(col, off)], half, m),
-                            half_of(ts[col].at[g, index(col, off)], half, m),
-                            par_send.at[s], par_recv.at[s], partner,
-                        ).start()
-
-    def rs_add(g, col, off, half, from_ring):
-        m = COLOURS[col][2]
-        own_part = half_of(ps[col].at[c, g, index(col, off)], half, m)
-        other = half_of(ts[col].at[g, index(col, off)], half, m)
-        wait_bytes(other, par_recv.at[par_sem(g, col, off, half)])
-        got = []
+    def head_parts(ref_of, g, hy):
+        hx = lax.rem(g + hy, 2)
+        return (
+            ref_of(0).at[:, pl.ds(hy * 2, 2)],
+            ref_of(1).at[pl.ds(hx * 2, 2), pl.ds((hy // 2) * NZ, NZ)],
+            ref_of(2).at[hy],
+        )
+
+    def to_partner(g, hy):
+        src = head_parts(lambda col: ps[col].at[1 - c, g], g, hy)
+        dst = head_parts(lambda col: ts[col].at[g], g, hy)
+        for col in range(3):
+            s = (g * 3 + col) * 4 + hy
+            remote(src[col], dst[col], par_send.at[s], par_recv.at[s], partner).start()
+
+    def from_partner(g):
+        for hy in range(NY):
+            dst = head_parts(lambda col: ts[col].at[g], g, hy)
+            for col in range(3):
+                wait_bytes(dst[col], par_recv.at[(g * 3 + col) * 4 + hy])
+
+    def add_parts(own_part, parts, count):
+        step = min(count, 4 if own_part.shape[-1] == 128 else 2)
+
+        @pl.loop(0, count // step)
+        def _(i):
+            rows = pl.ds(i * step, step)
+            v = own_part[rows].astype(F32)
+            for ref in parts:
+                v = v + ref[rows].astype(F32)
+            own_part[rows] = v.astype(BF16)
+
+    def rs_add(g, off, half, from_ring):
+        idx = lax.rem(z + off + NZ, NZ)
+        parts = [half_of(tz.at[g, idx], half)]
         for k, direction in from_ring:
-            s = ring_sem(g, col, k, direction, half)
-            wait_bytes(rings[col].at[s - BASE[col] - g * 32 + g * 2 * COLOURS[col][1]], rs_recv.at[s])
-            got.append(rings[col].at[s - BASE[col] - g * 32 + g * 2 * COLOURS[col][1]])
-
-        @pl.loop(0, m // 2)
-        def _(i):
-            v = own_part[i].astype(F32) + other[i].astype(F32)
-            for ref in got:
-                v = v + ref[i].astype(F32)
-            own_part[i] = v.astype(BF16)
+            s = ring_sem(g, k, direction, half)
+            wait_bytes(rz.at[s], rs_recv.at[s])
+            parts.append(rz.at[s])
+        add_parts(half_of(pz.at[c, g, idx], half), parts, ZM // 2)
 
     def rs_step(g, k):
-        for col in ORDER:
-            n, m = COLOURS[col][1:3]
-            top = n // 2
-
-            def part_step(half, direction, from_ring):
-                off = top - k if direction == 0 else k - top
-                rs_add(g, col, off, half, ((k - 1, direction),) if from_ring else ())
-                s = ring_sem(g, col, k, direction, half)
+        top = NZ // 2
+
+        def part_step(half, direction, from_ring):
+            off = top - k if direction == 0 else k - top
+            rs_add(g, off, half, ((k - 1, direction),) if from_ring else ())
+            s = ring_sem(g, k, direction, half)
+            remote(
+                half_of(pz.at[c, g, lax.rem(z + off + NZ, NZ)], half), rz.at[s],
+                rs_send.at[s], rs_recv.at[s], z_device(1 - 2 * direction),
+            ).start()
+
+        for half in (0, 1):
+            for direction in (0, 1):
+                first = 0 if half == direction else 1
+                when(k == first, lambda: part_step(half, direction, False))
+                if isinstance(k, int):
+                    when(first < k < top, lambda: part_step(half, direction, True))
+                else:
+                    pl.when((k > first) & (k < top))(lambda: part_step(half, direction, True))
+
+    def rs_send_xy(g):
+        for i in (2, 1, 3):
+            for col in (1, 2):
+                q, device = last_peer(col, i)
+                part = ps[col].at[c, g, q]
+                add_parts(part, [ts[col].at[g, q]], COLOURS[col][2])
+                s = last_sem(g, col, place[col])
                 remote(
-                    half_of(ps[col].at[c, g, index(col, off)], half, m),
-                    rings[col].at[s - BASE[col] - g * 32 + g * 2 * n],
-                    rs_send.at[s], rs_recv.at[s], ring_device(col, 1 - 2 * direction),
+                    part, rings[col].at[g, place[col]], rl_send.at[g * 2 + col - 1], rl_recv.at[s], device
                 ).start()
 
-            for half in (0, 1):
-                for direction in (0, 1):
-                    first = 0 if half == direction else 1
-                    when(k == first, lambda: part_step(half, direction, False))
-                    if isinstance(k, int):
-                        when(first < k < top, lambda: part_step(half, direction, True))
-                    elif first + 1 < top:
-                        pl.when((k > first) & (k < top))(lambda: part_step(half, direction, True))
-
-    def rs_lines(g):
-        for col in ORDER:
-            n = COLOURS[col][1]
-            for half in (0, 1):
-                rs_add(g, col, 0, half, tuple((n // 2 - 1, d) for d in (0, 1)))
+    def rs_take_xy(g):
+        for col in (1, 2):
+            parts = [ts[col].at[g, place[col]]]
+            for i in (1, 3, 2):
+                q = last_peer(col, i)[0]
+                wait_bytes(rings[col].at[g, q], rl_recv.at[last_sem(g, col, q)])
+                parts.append(rings[col].at[g, q])
+            add_parts(ps[col].at[c, g, place[col]], parts, COLOURS[col][2])
         for i in range(1, NY):
             q = y_peer(i)
             device = device_of(x, q, z, c)
@@ -403,6 +428,9 @@
                     py.at[c, g, y, pl.ds(lax.rem(q, 2) * NZ, NZ)], s1y.at[x], o1_send.at[1], o1_recv.at[1], device
                 ).start()
 
+    def rs_take_z(g):
+        for half in (0, 1):
+            rs_add(g, 0, half, tuple((NZ // 2 - 1, d) for d in (0, 1)))
         for i in range(1, NY):
             q = y_peer(i)
             remote(
@@ -410,65 +438,75 @@
                 device_of(x, q, z, c),
             ).start()
 
-    def sum_into(own_part, parts, count):
-        @pl.loop(0, count)
-        def _(i):
-            v = own_part[i].astype(F32)
-            for ref in parts:
-                v = v + ref[i].astype(F32)
-            own_part[i] = v.astype(BF16)
-
-    ag_start(0)
+    ag_start_z(0)
+    ag_start_xy(0)
+    send_rows()
     ag_step(0, 0)
     wait_bytes(tabs.at[c, 1 - x_lo], tab_recv.at[1])
     remote(tabs.at[c], tabs.at[c], tab_send.at[2], tab_recv.at[2], partner).start()
     ag_step(0, 1)
     ag_step(0, 2)
-    ag_start(1)
+    ag_start_z(1)
+    ag_start_xy(1)
+    ag_step(0, 3)
+    ag_take_xy(0)
     norm_rows()
-    ag_step(0, 3)
+    ag_step(1, 0)
     mask_rows()
     ag_done(0)
 
     @pl.loop(0, NY)
     def _(j):
         head(0, j)
-        ag_step(1, j)
-
-    rs_start(0)
+        to_partner(0, j)
+        pl.when(j < NY - 1)(lambda: ag_step(1, j + 1))
+        pl.when(j == 0)(lambda: ag_take_xy(1))
+
     ag_done(1)
 
     @pl.loop(0, NY)
     def _(j):
         head(1, j)
+        to_partner(1, j)
+
+        @pl.when(j == 0)
+        def _():
+            from_partner(0)
+            rs_send_xy(0)
+
         rs_step(0, j)
 
-    rs_start(1)
     rows_out()
+    from_partner(1)
+    rs_step(1, 0)
+    rs_send_xy(1)
     for i in range(1, HEADS):
         q = lax.rem(t + i, HEADS)
         remote(dr.at[q], grad_x.at[pl.ds(t * HIST, HIST)], out_send, out_recv, (u, q)).start()
     pltpu.make_async_copy(dr.at[t], grad_x.at[pl.ds(t * HIST, HIST)], loc.at[6]).start()
-    rs_lines(0)
-    for k in range(NZ // 2):
-        rs_step(1, k)
-    rs_lines(1)
+    rs_take_xy(0)
+    rs_take_z(0)
+    rs_step(1, 1)
+    rs_step(1, 2)
+    rs_step(1, 3)
+    rs_take_xy(1)
+    rs_take_z(1)
 
     wait_bytes(s1x.at[pl.ds(0, NY - 1)], o1_recv.at[0])
     line_px = px.at[c, mine, x, pl.ds((y // 2) * NZ, NZ)]
-    sum_into(line_px, [s1x.at[y_peer(i)] for i in range(1, NY)], NZ)
+    add_parts(line_px, [s1x.at[y_peer(i)] for i in range(1, NY)], NZ)
     for i in range(1, NZ):
         q = z_peer(i)
         remote(line_px.at[q], s2x.at[z], o2_send.at[1], o2_recv.at[1], device_of(x, y, q, c)).start()
     wait_bytes(s1y.at[pl.ds(0, NX - 1)], o1_recv.at[1])
     line_py = py.at[c, mine, y, pl.ds(x_lo * NZ, NZ)]
-    sum_into(line_py, [s1y.at[x_peer(i)] for i in range(1, NX)], NZ)
+    add_parts(line_py, [s1y.at[x_peer(i)] for i in range(1, NX)], NZ)
     for i in range(1, NZ):
         q = z_peer(i)
         remote(line_py.at[q], s2y.at[z], o2_send.at[2], o2_recv.at[2], device_of(x, y, q, c)).start()
     for g in range(2):
         wait_bytes(s1z.at[g, pl.ds(0, NY - 1)], o1z_recv.at[g])
-        sum_into(pz.at[c, g, z, pl.ds(y * 2, 2)], [s1z.at[g, y_peer(i)] for i in range(1, NY)], 2)
+        add_parts(pz.at[c, g, z, pl.ds(y * 2, 2)], [s1z.at[g, y_peer(i)] for i in range(1, NY)], 2)
     for i in range(1, NX):
         q = x_peer(i)
         remote(
@@ -512,19 +550,21 @@
         wait_bytes(ref.at[pl.ds(0, HEADS - 1)], a2a_send.at[k])
     for g in range(2):
         for col in range(3):
-            n, m = COLOURS[col][1:3]
             wait_bytes(gs[col].at[c, g], fw_send.at[g * 3 + col])
-            for half in (0, 1):
-                for direction in (0, 1):
-                    for k in range(n // 2):
-                        s = ring_sem(g, col, k, direction, half)
-                        part = half_of(gs[col].at[c, g, 0], half, m)
-                        if half == direction or k < n // 2 - 1:
-                            wait_bytes(part, ag_send.at[s])
-                        if half == direction or k > 0:
-                            wait_bytes(part, rs_send.at[s])
-                for off in range(n):
-                    wait_bytes(half_of(ts[col].at[g, 0], half, m), par_send.at[par_sem(g, col, off, half)])
+            for hy in range(NY):
+                dst = head_parts(lambda k: ts[k].at[g], g, hy)
+                wait_bytes(dst[col], par_send.at[(g * 3 + col) * 4 + hy])
+        for col in (1, 2):
+            wait_bytes(rings[col].at[g, pl.ds(0, 3)], last_send.at[g * 2 + col - 1])
+            wait_bytes(rings[col].at[g, pl.ds(0, 3)], rl_send.at[g * 2 + col - 1])
+        for half in (0, 1):
+            for direction in (0, 1):
+                for k in range(NZ // 2):
+                    s = ring_sem(g, k, direction, half)
+                    if half == direction or k < NZ // 2 - 1:
+                        wait_bytes(rz.at[s], ag_send.at[s])
+                    if half == direction or k > 0:
+                        wait_bytes(rz.at[s], rs_send.at[s])
     pltpu.make_async_copy(dr.at[t], grad_x.at[pl.ds(t * HIST, HIST)], loc.at[6]).wait()
     wait_bytes(dr.at[pl.ds(0, HEADS - 1)], out_send)
     wait_bytes(dr.at[pl.ds(0, HEADS - 1)], out_recv)
@@ -538,7 +578,7 @@
     dma = pltpu.SemaphoreType.DMA
     both = [pltpu.VMEM((2, 2, n, m, 32, w), BF16) for _, n, m, w in COLOURS]
     theirs = [pltpu.VMEM((2, n, m, 32, w), BF16) for _, n, m, w in COLOURS]
-    rings = [pltpu.VMEM((4 * n, m // 2, 32, w), BF16) for _, n, m, w in COLOURS]
+    rings = [pltpu.VMEM((32, ZM // 2, 32, 384), BF16)] + [pltpu.VMEM((2, n, m, 32, w), BF16) for _, n, m, w in COLOURS[1:]]
     lines = [
         pltpu.VMEM((2, NY, 2, 32, 384), BF16),
         pltpu.VMEM((NY, NZ, 32, 128), BF16),
@@ -565,8 +605,8 @@
     ]
     sems = [
         dma((7,)), dma((3,)), dma((3,)), dma((3,)), dma((2,)), dma((2,)), dma((NY,)), dma((NX,)),
-        dma((64,)), dma((64,)), dma((6,)), dma((6,)), dma((2,)), dma((2,)), dma((3,)), dma((3,)),
-        dma((64,)), dma((64,)), dma((64,)), dma((64,)),
+        dma((32,)), dma((32,)), dma((6,)), dma((6,)), dma((2,)), dma((2,)), dma((3,)), dma((3,)),
+        dma((24,)), dma((24,)), dma((32,)), dma((32,)), dma((4,)), dma((16,)), dma((4,)), dma((16,)),
         dma((2,)), dma((2,)), dma((2,)), dma((2,)), dma((3,)), dma((3,)), dma, dma,
     ]
     return pl.pallas_call(

time: 164 us -> 130 us (0.79)
  Pallas kernels: 158 us -> 124 us
    pallas_call x1, Pallas kernels: 158 us -> 124 us  [local(): pl.pallas_call(kernel, out_shape=(shape((32, SEQ, 128), BF16), shape((32,...]
where the time goes in v3:
time: 130 us; the launch traced here: 129 us
  Pallas kernels  124 us (95%)
  local copies, waits for them, and re-layouts  4.92 us (4%)
    pallas_call x1, Pallas kernels, local(): pl.pallas_call(kernel, out_shape=(shape((32, SEQ, 128), BF16), shape((32,...  124 us
    unnamed x11, local copies, waits for them, and re-layouts  4.32 us

profile of v3, /device:TPU:8, one launch (start us, length us, event | category | flops | bytes accessed | tf_op | source)
XLA Modules:
  0.0 129.2 jit_solution(13154979050815366649)
XLA Ops:
  0.6 0.0 copy-start.2
  0.6 0.0 copy-start.3
  0.7 0.6 copy-done.2
  1.3 0.0 copy-done.3
  1.3 0.6 pad.4.tab
  1.9 123.6 %step.1 = (bf16[32,128,128]{2,1,0:T(8,128)(2,1)}, f32[32,512]{1,0:T(8,128)}, f32[32,128]{1,0:T(8,128)}) custom-call(bf16[32,128,128]{2,1,0:T(8,128)(2,1)} %ev.1, bf16[32,128,128]{2,1,0:T(8,128)(2,1)} %ct.1, bf16[32,512]{1,0:T(8,128)(2,1)} %w_in.1, bf16[32,128]{1,0:T(8,128)(2,1)} %w_out.1, s32[8,128]{1,0:T(8,128)} %pad.4.tab), custom_call_target="tpu_custom_call" | custom-call | tf_op jit(solution)/shard_map/step/pallas_call | solution.py:612
  125.6 0.0 copy-start
  125.6 2.3 %copy.12 = bf16[32,128,128]{2,1,0:T(8,128)(2,1)} copy(bf16[32,128,128]{2,1,0:T(8,128)(2,1)} %get-tuple-element.6) | data formatting | bytes 2097152
  127.9 0.0 copy-done
  127.9 0.0 copy-start.1
  127.9 0.6 copy.13
  128.6 0.1 copy-done.1
  128.6 0.6 copy.14
  (1 shorter events, 0.0 us)
Async XLA Ops:
  0.6 0.7 copy-start.2
  0.6 0.7 copy-start.3
  125.6 2.4 %copy-start = (f32[32,512]{1,0:T(8,128)S(1)}, f32[32,512]{1,0:T(8,128)}, u32[]{:S(2)}) copy-start(f32[32,512]{1,0:T(8,128)} %get-tuple-element.7) | copy-start | bytes 196612
  127.9 0.7 copy-start.1

commit v4 on v3

--- a/solution.py
+++ b/solution.py
@@ -58,7 +58,7 @@
 def kernel(
     ev, ct, w_in, w_out, tab, grad_x, grad_wi, grad_wo,
     gz, gx, gy, pz, px, py, tz, tx, ty, rz, rx, ry, s1z, s1x, s1y, s2z, s2x, s2y,
-    xr, dr, tabs, nf, nb, nbt, dm, dmt, rstd_s, dn, wh, wo, dz_s, hb_s,
+    xr, dr, tabs, nf, nb, nbt, dm, dmt, rstd_s, dn, wh, wo, dz_s, hb_s, z_s,
     loc, st1_send, st1_recv, st2_send, z2_send, z2_recv, x2_recv, y2_recv, ag_send, ag_recv, fw_send, fw_recv,
     a2a_send, a2a_recv, tab_send, tab_recv, par_send, par_recv, rs_send, rs_recv,
     last_send, last_recv, rl_send, rl_recv,
@@ -107,6 +107,13 @@
     for i in range(1, NZ):
         greet(device_of(x, y, z_peer(i), c))
     pl.semaphore_wait(barrier, 17)
+
+    def send_rows(k):
+        src, dst = ((ev, xr), (ct, dr))[k]
+        pltpu.make_async_copy(src.at[pl.ds(t * HIST, HIST)], dst.at[t], loc.at[4 + k]).start()
+        for i in range(1, HEADS):
+            q = lax.rem(t + i, HEADS)
+            remote(src.at[pl.ds(q * HIST, HIST)], dst.at[t], a2a_send.at[k], a2a_recv.at[k], (u, q)).start()
 
     pieces = (w_in.at[:, pl.ds(0, 384)], w_in.at[:, pl.ds(384, 128)], w_out)
     slots = (
@@ -136,6 +143,7 @@
 
     wait_bytes(gz.at[c, 0, z, pl.ds(0, NX - 1)], st1_recv.at[0])
     line_z(0)
+    line_z(1)
     line_x = gx.at[c, mine, x, pl.ds((y // 2) * NZ, NZ)]
     line_y = gy.at[c, mine, y, pl.ds(x_lo * NZ, NZ)]
     wait_bytes(gx.at[c, mine, x, pl.ds(0, NZ - 1)], st1_recv.at[1])
@@ -144,14 +152,6 @@
     wait_bytes(gy.at[c, mine, y, pl.ds(0, NZ - 1)], st1_recv.at[2])
     for i in range(1, NX):
         remote(line_y, line_y, st2_send.at[2], y2_recv.at[x], device_of(x_peer(i), y, z, c)).start()
-    line_z(1)
-
-    def send_rows():
-        for k, (src, dst) in enumerate(((ev, xr), (ct, dr))):
-            pltpu.make_async_copy(src.at[pl.ds(t * HIST, HIST)], dst.at[t], loc.at[4 + k]).start()
-            for i in range(1, HEADS):
-                q = lax.rem(t + i, HEADS)
-                remote(src.at[pl.ds(q * HIST, HIST)], dst.at[t], a2a_send.at[k], a2a_recv.at[k], (u, q)).start()
 
     wait_bytes(tabs.at[c, x_lo, pl.ds(0, NZ - 1)], tab_recv.at[0])
     rows_tab = tabs.at[c, x_lo]
@@ -264,57 +264,112 @@
             dmt[:, rows] = di.T
         dn[...] = jnp.zeros_like(dn)
 
-    def head(g, hy):
-        hx = lax.rem(g + hy, 2)
-        for xl in range(2):
-            for zz in range(NZ):
-                for cc in range(2):
-                    r = pl.ds(((xl * NZ + zz) * 2 + cc) * 32, 32)
-                    wh[r, pl.ds(0, 384)] = gz[cc, g, zz, hy * 2 + xl]
-                    wh[r, pl.ds(384, 128)] = gx[cc, g, hx * 2 + xl, (hy // 2) * NZ + zz]
-                    wo[r, :] = gy[cc, g, hy, xl * NZ + zz]
-        scale = HD ** (-0.5)
-        zv = dot(nb[...], wh[...], NN)
+    scale = HD ** (-0.5)
+    hs = [slice(i * SEQ, i * SEQ + SEQ) for i in range(HIST)]
+    causal_one = lax.broadcasted_iota(jnp.int32, (SEQ, SEQ), 1) <= lax.broadcasted_iota(jnp.int32, (SEQ, SEQ), 0)
+
+    def each(f):
+        return jnp.concatenate([f(r) for r in hs], axis=0)
+
+    def attention(zv, grad_h, k):
         gv, sg = silu_parts(zv)
         gv = gv.astype(BF16)
-        grad_h = dot(dm[...], wo[...], NN)
         uf = gv[:, 0:128].astype(F32)
         vp, qp, kp = gv[:, 128:256], gv[:, 256:384], gv[:, 384:512]
-        hs = [slice(i * SEQ, i * SEQ + SEQ) for i in range(HIST)]
-
-        def each(f):
-            return jnp.concatenate([f(r) for r in hs], axis=0)
-
+        yield
         s = each(lambda r: dot(qp[r], kp[r], NT)) * scale
-        causal = lax.broadcasted_iota(jnp.int32, (SEQ, SEQ), 1) <= lax.broadcasted_iota(jnp.int32, (SEQ, SEQ), 0)
-        causal = jnp.concatenate([causal] * HIST, axis=0)
+        causal = jnp.concatenate([causal_one] * HIST, axis=0)
         ss, sgs = silu_parts(s)
         at = jnp.where(causal, ss / SEQ, 0.0).astype(BF16)
+        yield
         yv = each(lambda r: dot(at[r], vp[r], NN))
         ycen = yv - jnp.mean(yv, axis=1, keepdims=True)
+        yield
         yrstd = lax.rsqrt(jnp.mean(ycen * ycen, axis=1, keepdims=True) + EPS)
         yn = ycen * yrstd
-        hb_s[...] = (yn * uf).astype(BF16)
-        dz_s[:, 0:128] = (grad_h * yn * sg[:, 0:128]).astype(BF16)
+        hb_s[:, k * 128 : k * 128 + 128] = (yn * uf).astype(BF16)
+        dz_s[:, k * 512 : k * 512 + 128] = (grad_h * yn * sg[:, 0:128]).astype(BF16)
+        yield
         gyn = grad_h * uf
         dy = (
             (gyn - jnp.mean(gyn, axis=1, keepdims=True) - yn * jnp.mean(gyn * yn, axis=1, keepdims=True)) * yrstd
         ).astype(BF16)
+        yield
         da = each(lambda r: dot(dy[r], vp[r], NT))
-        dz_s[:, 128:256] = (each(lambda r: dot(at[r], dy[r], TN)) * sg[:, 128:256]).astype(BF16)
+        dz_s[:, k * 512 + 128 : k * 512 + 256] = (each(lambda r: dot(at[r], dy[r], TN)) * sg[:, 128:256]).astype(BF16)
+        yield
         ds_ = jnp.where(causal, da * sgs * (scale / SEQ), 0.0).astype(BF16)
-        dz_s[:, 256:384] = (each(lambda r: dot(ds_[r], kp[r], NN)) * sg[:, 256:384]).astype(BF16)
-        dz_s[:, 384:512] = (each(lambda r: dot(ds_[r], qp[r], TN)) * sg[:, 384:512]).astype(BF16)
+        yield
+        dz_s[:, k * 512 + 256 : k * 512 + 384] = (each(lambda r: dot(ds_[r], kp[r], NN)) * sg[:, 256:384]).astype(BF16)
+        dz_s[:, k * 512 + 384 : k * 512 + 512] = (each(lambda r: dot(ds_[r], qp[r], TN)) * sg[:, 384:512]).astype(BF16)
+
+    def beside(stages, others):
+        others = list(others)
+        for _ in stages:
+            if others:
+                others.pop(0)()
+        for other in others:
+            other()
+
+    def pair(g, yy, middle):
+        for k in range(2):
+            hy = 2 * yy + k
+            hx = lax.rem(g + hy, 2)
+            for xl in range(2):
+                for zz in range(NZ):
+                    for cc in range(2):
+                        r = pl.ds(((xl * NZ + zz) * 2 + cc) * 32, 32)
+                        wh[r, pl.ds(k * 512, 384)] = gz[cc, g, zz, hy * 2 + xl]
+                        wh[r, pl.ds(k * 512 + 384, 128)] = gx[cc, g, hx * 2 + xl, yy * NZ + zz]
+                        wo[r, pl.ds(k * 128, 128)] = gy[cc, g, hy, xl * NZ + zz]
+
+        def z_rows(i):
+            def run():
+                rows = pl.ds(i * 64, 64)
+                z_s[rows, :] = dot(nb[rows, :], wh[:, 512:1024], NN)
+
+            return run
+
+        def out_of(k, j):
+            hy = 2 * yy + k
+            hx = lax.rem(g + hy, 2)
+
+            def weights():
+                gw = dot(nbt[pl.ds(j * 256, 256), :], dz_s[:, k * 512 : k * 512 + 512], NN).astype(BF16)
+                for i in range(8):
+                    uu = j * 8 + i
+                    cc, zz, xl = uu % 2, (uu // 2) % NZ, uu // (2 * NZ)
+                    pz[cc, g, zz, hy * 2 + xl] = gw[i * 32 : i * 32 + 32, 0:384]
+                    px[cc, g, hx * 2 + xl, yy * NZ + zz] = gw[i * 32 : i * 32 + 32, 384:512]
+
+            def rows():
+                dn[:, pl.ds(j * 256, 256)] += dot(
+                    dz_s[:, k * 512 : k * 512 + 512], wh[pl.ds(j * 256, 256), k * 512 : k * 512 + 512], NT
+                )
+
+            return [weights, rows]
+
+        def both(j):
+            def run():
+                go = dot(dmt[pl.ds(j * 256, 256), :], hb_s[...], NN).astype(BF16)
+                for i in range(8):
+                    uu = j * 8 + i
+                    cc, zz, xl = uu % 2, (uu // 2) % NZ, uu // (2 * NZ)
+                    for k in range(2):
+                        py[cc, g, 2 * yy + k, xl * NZ + zz] = go[i * 32 : i * 32 + 32, k * 128 : k * 128 + 128]
+
+            return run
+
+        z0 = dot(nb[...], wh[:, 0:512], NN)
+        grad_h = dot(dm[...], wo[...], NN)
+        beside(attention(z0, grad_h[:, 0:128], 0), [z_rows(i) for i in range(8)])
+        middle()
+        first = [f for j in range(4) for f in out_of(0, j)]
+        beside(attention(z_s[...], grad_h[:, 128:256], 1), first)
         for j in range(4):
-            gw = dot(nbt[pl.ds(j * 256, 256), :], dz_s[...], NN).astype(BF16)
-            go = dot(dmt[pl.ds(j * 256, 256), :], hb_s[...], NN).astype(BF16)
-            for k in range(8):
-                uu = j * 8 + k
-                cc, zz, xl = uu % 2, (uu // 2) % NZ, uu // (2 * NZ)
-                pz[cc, g, zz, hy * 2 + xl] = gw[k * 32 : k * 32 + 32, 0:384]
-                px[cc, g, hx * 2 + xl, (hy // 2) * NZ + zz] = gw[k * 32 : k * 32 + 32, 384:512]
-                py[cc, g, hy, xl * NZ + zz] = go[k * 32 : k * 32 + 32, :]
-            dn[:, pl.ds(j * 256, 256)] += dot(dz_s[...], wh[pl.ds(j * 256, 256), :], NT)
+            both(j)()
+            for f in out_of(1, j):
+                f()
 
     def rows_out():
         for i in range(HIST):
@@ -342,8 +397,9 @@
             s = (g * 3 + col) * 4 + hy
             remote(src[col], dst[col], par_send.at[s], par_recv.at[s], partner).start()
 
-    def from_partner(g):
-        for hy in range(NY):
+    def from_partner(part):
+        g = part // 2
+        for hy in (part % 2 * 2, part % 2 * 2 + 1):
             dst = head_parts(lambda col: ts[col].at[g], g, hy)
             for col in range(3):
                 wait_bytes(dst[col], par_recv.at[(g * 3 + col) * 4 + hy])
@@ -359,65 +415,78 @@
                 v = v + ref[rows].astype(F32)
             own_part[rows] = v.astype(BF16)
 
-    def rs_add(g, off, half, from_ring):
+    def rz_half(ref, yy, half):
+        return ref.at[pl.ds(yy * 4 + half * 2, 2)]
+
+    def rs_sem(part, k, direction, half):
+        return part * 16 + (direction * (NZ // 2) + k) * 2 + half
+
+    def rs_add(part, off, half, from_ring):
+        g, yy = part // 2, part % 2
         idx = lax.rem(z + off + NZ, NZ)
-        parts = [half_of(tz.at[g, idx], half)]
+        parts = [rz_half(tz.at[g, idx], yy, half)]
         for k, direction in from_ring:
-            s = ring_sem(g, k, direction, half)
+            s = rs_sem(part, k, direction, half)
             wait_bytes(rz.at[s], rs_recv.at[s])
             parts.append(rz.at[s])
-        add_parts(half_of(pz.at[c, g, idx], half), parts, ZM // 2)
-
-    def rs_step(g, k):
-        top = NZ // 2
-
-        def part_step(half, direction, from_ring):
-            off = top - k if direction == 0 else k - top
-            rs_add(g, off, half, ((k - 1, direction),) if from_ring else ())
-            s = ring_sem(g, k, direction, half)
-            remote(
-                half_of(pz.at[c, g, lax.rem(z + off + NZ, NZ)], half), rz.at[s],
-                rs_send.at[s], rs_recv.at[s], z_device(1 - 2 * direction),
-            ).start()
-
+        add_parts(rz_half(pz.at[c, g, idx], yy, half), parts, 2)
+
+    def rs_step(part, k):
+        g, yy = part // 2, part % 2
         for half in (0, 1):
             for direction in (0, 1):
-                first = 0 if half == direction else 1
-                when(k == first, lambda: part_step(half, direction, False))
-                if isinstance(k, int):
-                    when(first < k < top, lambda: part_step(half, direction, True))
-                else:
-                    pl.when((k > first) & (k < top))(lambda: part_step(half, direction, True))
-
-    def rs_send_xy(g):
+                if k == 0 and half != direction:
+                    continue
+                off = NZ // 2 - k if direction == 0 else k - NZ // 2
+                rs_add(part, off, half, ((k - 1, direction),) if k > 1 or (k == 1 and half == direction) else ())
+                s = rs_sem(part, k, direction, half)
+                remote(
+                    rz_half(pz.at[c, g, lax.rem(z + off + NZ, NZ)], yy, half), rz.at[s],
+                    rs_send.at[s], rs_recv.at[s], z_device(1 - 2 * direction),
+                ).start()
+
+    def send_x(part):
+        g, yy = part // 2, part % 2
+        sub = pl.ds(yy * NZ, NZ)
         for i in (2, 1, 3):
-            for col in (1, 2):
-                q, device = last_peer(col, i)
-                part = ps[col].at[c, g, q]
-                add_parts(part, [ts[col].at[g, q]], COLOURS[col][2])
-                s = last_sem(g, col, place[col])
-                remote(
-                    part, rings[col].at[g, place[col]], rl_send.at[g * 2 + col - 1], rl_recv.at[s], device
-                ).start()
-
-    def rs_take_xy(g):
-        for col in (1, 2):
-            parts = [ts[col].at[g, place[col]]]
-            for i in (1, 3, 2):
-                q = last_peer(col, i)[0]
-                wait_bytes(rings[col].at[g, q], rl_recv.at[last_sem(g, col, q)])
-                parts.append(rings[col].at[g, q])
-            add_parts(ps[col].at[c, g, place[col]], parts, COLOURS[col][2])
+            q, device = last_peer(1, i)
+            add_parts(px.at[c, g, q, sub], [tx.at[g, q, sub]], NZ)
+            remote(
+                px.at[c, g, q, sub], rx.at[g, x, sub], rl_send.at[part], rl_recv.at[part * 4 + x], device
+            ).start()
+
+    def send_y(g):
+        for i in (2, 1, 3):
+            q, device = last_peer(2, i)
+            add_parts(py.at[c, g, q], [ty.at[g, q]], 16)
+            remote(
+                py.at[c, g, q], ry.at[g, y], rl_send.at[4 + g], rl_recv.at[16 + g * 4 + y], device
+            ).start()
+
+    def take_x(part):
+        g, yy = part // 2, part % 2
+        sub = pl.ds(yy * NZ, NZ)
+        parts = [tx.at[g, x, sub]]
+        for i in (1, 3, 2):
+            q = x_peer(i)
+            wait_bytes(rx.at[g, q, sub], rl_recv.at[part * 4 + q])
+            parts.append(rx.at[g, q, sub])
+        add_parts(px.at[c, g, x, sub], parts, NZ)
         for i in range(1, NY):
             q = y_peer(i)
             device = device_of(x, q, z, c)
 
-            @pl.when(lax.rem(q + x_hi, 2) == g)
+            @pl.when((lax.rem(q + x_hi, 2) == g) & (q // 2 == yy))
             def _():
-                remote(
-                    px.at[c, g, x, pl.ds((q // 2) * NZ, NZ)], s1x.at[y], o1_send.at[0], o1_recv.at[0], device
-                ).start()
-
+                remote(px.at[c, g, x, sub], s1x.at[y], o1_send.at[0], o1_recv.at[0], device).start()
+
+    def take_y(g):
+        parts = [ty.at[g, y]]
+        for i in (1, 3, 2):
+            q = y_peer(i)
+            wait_bytes(ry.at[g, q], rl_recv.at[16 + g * 4 + q])
+            parts.append(ry.at[g, q])
+        add_parts(py.at[c, g, y], parts, 16)
         for i in range(1, NX):
             q = x_peer(i)
             device = device_of(q, y, z, c)
@@ -428,69 +497,117 @@
                     py.at[c, g, y, pl.ds(lax.rem(q, 2) * NZ, NZ)], s1y.at[x], o1_send.at[1], o1_recv.at[1], device
                 ).start()
 
-    def rs_take_z(g):
+    def take_z(part):
+        g, yy = part // 2, part % 2
         for half in (0, 1):
-            rs_add(g, 0, half, tuple((NZ // 2 - 1, d) for d in (0, 1)))
+            rs_add(part, 0, half, tuple((NZ // 2 - 1, d) for d in (0, 1)))
         for i in range(1, NY):
             q = y_peer(i)
-            remote(
-                pz.at[c, g, z, pl.ds(q * 2, 2)], s1z.at[g, y], o1z_send.at[g], o1z_recv.at[g],
-                device_of(x, q, z, c),
-            ).start()
+            device = device_of(x, q, z, c)
+
+            @pl.when(q // 2 == yy)
+            def _():
+                remote(
+                    pz.at[c, g, z, pl.ds(q * 2, 2)], s1z.at[g, y], o1z_send.at[g], o1z_recv.at[g], device
+                ).start()
 
     ag_start_z(0)
+    ag_start_z(1)
     ag_start_xy(0)
-    send_rows()
+    send_rows(0)
+    send_rows(1)
     ag_step(0, 0)
     wait_bytes(tabs.at[c, 1 - x_lo], tab_recv.at[1])
     remote(tabs.at[c], tabs.at[c], tab_send.at[2], tab_recv.at[2], partner).start()
+    ag_step(1, 0)
+    ag_start_xy(1)
     ag_step(0, 1)
+    ag_step(1, 1)
     ag_step(0, 2)
-    ag_start_z(1)
-    ag_start_xy(1)
-    ag_step(0, 3)
+    ag_step(1, 2)
     ag_take_xy(0)
     norm_rows()
-    ag_step(1, 0)
+    ag_step(0, 3)
+    ag_step(1, 3)
     mask_rows()
     ag_done(0)
 
-    @pl.loop(0, NY)
+    @pl.loop(0, 2)
     def _(j):
-        head(0, j)
-        to_partner(0, j)
-        pl.when(j < NY - 1)(lambda: ag_step(1, j + 1))
-        pl.when(j == 0)(lambda: ag_take_xy(1))
+        def middle():
+            @pl.when(j == 0)
+            def _():
+                ag_take_xy(1)
+
+            @pl.when(j == 1)
+            def _():
+                from_partner(0)
+                rs_step(0, 0)
+                send_x(0)
+
+        pair(0, j, middle)
+        to_partner(0, 2 * j)
+        to_partner(0, 2 * j + 1)
+        pl.when(j == 1)(lambda: rs_step(0, 1))
 
     ag_done(1)
 
-    @pl.loop(0, NY)
+    @pl.loop(0, 2)
     def _(j):
-        head(1, j)
-        to_partner(1, j)
+        def middle():
+            @pl.when(j == 0)
+            def _():
+                rs_step(0, 2)
+                from_partner(1)
+                rs_step(1, 0)
+                send_x(1)
+                send_y(0)
+
+            @pl.when(j == 1)
+            def _():
+                rs_step(1, 2)
+                from_partner(2)
+                rs_step(2, 0)
+                send_x(2)
+                take_z(0)
+                take_x(0)
+
+        pair(1, j, middle)
+        to_partner(1, 2 * j)
+        to_partner(1, 2 * j + 1)
 
         @pl.when(j == 0)
         def _():
-            from_partner(0)
-            rs_send_xy(0)
-
-        rs_step(0, j)
+            rs_step(0, 3)
+            rs_step(1, 1)
+
+        @pl.when(j == 1)
+        def _():
+            rs_step(1, 3)
+            rs_step(2, 1)
 
     rows_out()
-    from_partner(1)
-    rs_step(1, 0)
-    rs_send_xy(1)
     for i in range(1, HEADS):
         q = lax.rem(t + i, HEADS)
         remote(dr.at[q], grad_x.at[pl.ds(t * HIST, HIST)], out_send, out_recv, (u, q)).start()
     pltpu.make_async_copy(dr.at[t], grad_x.at[pl.ds(t * HIST, HIST)], loc.at[6]).start()
-    rs_take_xy(0)
-    rs_take_z(0)
-    rs_step(1, 1)
-    rs_step(1, 2)
-    rs_step(1, 3)
-    rs_take_xy(1)
-    rs_take_z(1)
+    from_partner(3)
+    rs_step(3, 0)
+    send_x(3)
+    send_y(1)
+    rs_step(2, 2)
+    take_z(1)
+    take_x(1)
+    take_y(0)
+    rs_step(3, 1)
+    rs_step(2, 3)
+    rs_step(3, 2)
+    take_z(2)
+    take_x(2)
+    rs_step(3, 3)
+    take_x(3)
+    take_y(1)
+    take_z(3)
 
     wait_bytes(s1x.at[pl.ds(0, NY - 1)], o1_recv.at[0])
     line_px = px.at[c, mine, x, pl.ds((y // 2) * NZ, NZ)]
@@ -556,15 +673,19 @@
                 wait_bytes(dst[col], par_send.at[(g * 3 + col) * 4 + hy])
         for col in (1, 2):
             wait_bytes(rings[col].at[g, pl.ds(0, 3)], last_send.at[g * 2 + col - 1])
-            wait_bytes(rings[col].at[g, pl.ds(0, 3)], rl_send.at[g * 2 + col - 1])
         for half in (0, 1):
             for direction in (0, 1):
                 for k in range(NZ // 2):
                     s = ring_sem(g, k, direction, half)
                     if half == direction or k < NZ // 2 - 1:
-                        wait_bytes(rz.at[s], ag_send.at[s])
+                        wait_bytes(block(g, 0, half), ag_send.at[s])
                     if half == direction or k > 0:
-                        wait_bytes(rz.at[s], rs_send.at[s])
+                        for part in (2 * g, 2 * g + 1):
+                            s = rs_sem(part, k, direction, half)
+                            wait_bytes(rz.at[s], rs_send.at[s])
+        wait_bytes(ry.at[g, pl.ds(0, 3)], rl_send.at[4 + g])
+        for part in (2 * g, 2 * g + 1):
+            wait_bytes(rx.at[g, pl.ds(0, 3), pl.ds(0, NZ)], rl_send.at[part])
     pltpu.make_async_copy(dr.at[t], grad_x.at[pl.ds(t * HIST, HIST)], loc.at[6]).wait()
     wait_bytes(dr.at[pl.ds(0, HEADS - 1)], out_send)
     wait_bytes(dr.at[pl.ds(0, HEADS - 1)], out_recv)
@@ -578,7 +699,7 @@
     dma = pltpu.SemaphoreType.DMA
     both = [pltpu.VMEM((2, 2, n, m, 32, w), BF16) for _, n, m, w in COLOURS]
     theirs = [pltpu.VMEM((2, n, m, 32, w), BF16) for _, n, m, w in COLOURS]
-    rings = [pltpu.VMEM((32, ZM // 2, 32, 384), BF16)] + [pltpu.VMEM((2, n, m, 32, w), BF16) for _, n, m, w in COLOURS[1:]]
+    rings = [pltpu.VMEM((64, 2, 32, 384), BF16)] + [pltpu.VMEM((2, n, m, 32, w), BF16) for _, n, m, w in COLOURS[1:]]
     lines = [
         pltpu.VMEM((2, NY, 2, 32, 384), BF16),
         pltpu.VMEM((NY, NZ, 32, 128), BF16),
@@ -598,15 +719,16 @@
         pltpu.VMEM((D, ROWS), BF16),
         pltpu.VMEM((ROWS, 128), F32),
         pltpu.VMEM((ROWS, D), F32),
-        pltpu.VMEM((D, 512), BF16),
-        pltpu.VMEM((D, 128), BF16),
-        pltpu.VMEM((ROWS, 512), BF16),
-        pltpu.VMEM((ROWS, 128), BF16),
+        pltpu.VMEM((D, 1024), BF16),
+        pltpu.VMEM((D, 256), BF16),
+        pltpu.VMEM((ROWS, 1024), BF16),
+        pltpu.VMEM((ROWS, 256), BF16),
+        pltpu.VMEM((ROWS, 512), F32),
     ]
     sems = [
         dma((7,)), dma((3,)), dma((3,)), dma((3,)), dma((2,)), dma((2,)), dma((NY,)), dma((NX,)),
         dma((32,)), dma((32,)), dma((6,)), dma((6,)), dma((2,)), dma((2,)), dma((3,)), dma((3,)),
-        dma((24,)), dma((24,)), dma((32,)), dma((32,)), dma((4,)), dma((16,)), dma((4,)), dma((16,)),
+        dma((24,)), dma((24,)), dma((64,)), dma((64,)), dma((4,)), dma((16,)), dma((6,)), dma((24,)),
         dma((2,)), dma((2,)), dma((2,)), dma((2,)), dma((3,)), dma((3,)), dma, dma,
     ]
     return pl.pallas_call(

time: 130 us -> 128 us (0.985); the launches traced: 129 us -> 126 us
  Pallas kernels: 124 us -> 120 us
    pallas_call x1, Pallas kernels: 124 us -> 120 us  [local(): pl.pallas_call(kernel, out_shape=(shape((32, SEQ, 128), BF16), shape((32,...]
where the time goes in v4:
time: 128 us; the launch traced here: 126 us
  Pallas kernels  120 us (94%)
  local copies, waits for them, and re-layouts  4.92 us (4%)
    pallas_call x1, Pallas kernels, local(): pl.pallas_call(kernel, out_shape=(shape((32, SEQ, 128), BF16), shape((32,...  120 us
    unnamed x11, local copies, waits for them, and re-layouts  4.32 us

profile of v4, /device:TPU:8, one launch (start us, length us, event | category | flops | bytes accessed | tf_op | source)
XLA Modules:
  0.0 125.5 jit_solution(1164357187521878170)
XLA Ops:
  0.6 0.0 copy-start.2
  0.6 0.0 copy-start.3
  0.7 0.6 copy-done.2
  1.3 0.0 copy-done.3
  1.3 0.6 pad.4.tab
  1.9 119.9 %step.1 = (bf16[32,128,128]{2,1,0:T(8,128)(2,1)}, f32[32,512]{1,0:T(8,128)}, f32[32,128]{1,0:T(8,128)}) custom-call(bf16[32,128,128]{2,1,0:T(8,128)(2,1)} %ev.1, bf16[32,128,128]{2,1,0:T(8,128)(2,1)} %ct.1, bf16[32,512]{1,0:T(8,128)(2,1)} %w_in.1, bf16[32,128]{1,0:T(8,128)(2,1)} %w_out.1, s32[8,128]{1,0:T(8,128)} %pad.4.tab), custom_call_target="tpu_custom_call" | custom-call | tf_op jit(solution)/shard_map/step/pallas_call | solution.py:734
  121.9 0.0 copy-start
  121.9 2.3 %copy.12 = bf16[32,128,128]{2,1,0:T(8,128)(2,1)} copy(bf16[32,128,128]{2,1,0:T(8,128)(2,1)} %get-tuple-element.6) | data formatting | bytes 2097152
  124.2 0.0 copy-done
  124.2 0.0 copy-start.1
  124.2 0.6 copy.13
  124.9 0.1 copy-done.1
  124.9 0.6 copy.14
  (1 shorter events, 0.0 us)
Async XLA Ops:
  0.6 0.7 copy-start.2
  0.6 0.7 copy-start.3
  121.9 2.4 %copy-start = (f32[32,512]{1,0:T(8,128)S(1)}, f32[32,512]{1,0:T(8,128)}, u32[]{:S(2)}) copy-start(f32[32,512]{1,0:T(8,128)} %get-tuple-element.7) | copy-start | bytes 196612
  124.2 0.7 copy-start.1

commit v5 on v4

--- a/solution.py
+++ b/solution.py
@@ -691,6 +691,12 @@
     wait_bytes(dr.at[pl.ds(0, HEADS - 1)], out_recv)
 
 
+def hand_out(a, b, c, out_a, out_b, out_c):
+    out_a[...] = a[...]
+    out_b[...] = b[...]
+    out_c[...] = c[...]
+
+
 def local(events, cotangent, w_in, w_out, slot_source, slot_length):
     tab = jnp.pad(jnp.stack([slot_source, slot_length]), ((0, 6), (0, 96)))
     any_ = pl.BlockSpec(memory_space=pl.ANY)
@@ -731,10 +737,10 @@
         dma((24,)), dma((24,)), dma((64,)), dma((64,)), dma((4,)), dma((16,)), dma((6,)), dma((24,)),
         dma((2,)), dma((2,)), dma((2,)), dma((2,)), dma((3,)), dma((3,)), dma, dma,
     ]
-    return pl.pallas_call(
+    found = pl.pallas_call(
         kernel,
         out_shape=(shape((32, SEQ, 128), BF16), shape((32, 512), F32), shape((32, 128), F32)),
-        in_specs=[any_, any_, vmem, vmem, vmem],
+        in_specs=[any_, any_, any_, any_, any_],
         out_specs=(any_, vmem, vmem),
         scratch_shapes=both + both + theirs + rings + lines + work + sems,
         compiler_params=pltpu.CompilerParams(
@@ -742,6 +748,19 @@
         ),
         name="step",
     )(events, cotangent, w_in, w_out, tab)
+    specs = [
+        pl.BlockSpec((8, SEQ, 128), lambda i: (i, 0, 0)),
+        pl.BlockSpec((8, 512), lambda i: (i, 0)),
+        pl.BlockSpec((8, 128), lambda i: (i, 0)),
+    ]
+    return pl.pallas_call(
+        hand_out,
+        grid=(4,),
+        out_shape=tuple(shape(f.shape, f.dtype) for f in found),
+        in_specs=specs,
+        out_specs=tuple(specs),
+        name="hand_out",
+    )(*found)
 
 
 def solution(mesh):

time: 128 us -> 126 us (0.984); the launches traced: 126 us -> 125 us
  local copies, waits for them, and re-layouts: 4.92 us -> 1.26 us
  Pallas kernels: 120 us -> 123 us
    unnamed x11 -> x4, local copies, waits for them, and re-layouts: 4.32 us -> 0.66 us
    pallas_call x0 -> x1, Pallas kernels: none -> 3.42 us  [local(): pl.pallas_call(hand_out, grid=(4,), out_shape=tuple((shape(f.shape, f.dty...]
where the time goes in v5:
time: 126 us; the launch traced here: 125 us
  Pallas kernels  123 us (98%)
  local copies, waits for them, and re-layouts  1.26 us (1%)
    pallas_call x1, Pallas kernels, local(): pl.pallas_call(kernel, out_shape=(shape((32, SEQ, 128), BF16), shape((32,...  120 us
    pallas_call x1, Pallas kernels, local(): pl.pallas_call(hand_out, grid=(4,), out_shape=tuple((shape(f.shape, f.dty...  3.42 us

profile of v5, /device:TPU:8, one launch (start us, length us, event | category | flops | bytes accessed | tf_op | source)
XLA Modules:
  0.0 125.3 jit_solution(13773417217956763134)
XLA Ops:
  0.6 0.0 copy-start
  0.6 0.0 copy-start.1
  0.7 0.6 copy-done
  1.3 0.0 copy-done.1
  1.3 0.6 pad.4.tab
  1.9 120.0 %step.1 = (bf16[32,128,128]{2,1,0:T(8,128)(2,1)}, f32[32,512]{1,0:T(8,128)}, f32[32,128]{1,0:T(8,128)}) custom-call(bf16[32,128,128]{2,1,0:T(8,128)(2,1)} %ev.1, bf16[32,128,128]{2,1,0:T(8,128)(2,1)} %ct.1, bf16[32,512]{1,0:T(8,128)(2,1)} %w_in.1, bf16[32,128]{1,0:T(8,128)(2,1)} %w_out.1, s32[8,128]{1,0:T(8,128)} %pad.4.tab), custom_call_target="tpu_custom_call" | custom-call | tf_op jit(solution)/shard_map/step/pallas_call | solution.py:740
  121.9 3.4 %hand_out.1 = (bf16[32,128,128]{2,1,0:T(8,128)(2,1)}, f32[32,512]{1,0:T(8,128)}, f32[32,128]{1,0:T(8,128)}) custom-call(bf16[32,128,128]{2,1,0:T(8,128)(2,1)} %get-tuple-element.6.a, f32[32,512]{1,0:T(8,128)} %get-tuple-element.7.b, f32[32,128]{1,0:T(8,128)} %get-tuple-element.8.c), custom_call_target="tpu_custom_call" | custom-call | tf_op jit(solution)/shard_map/hand_out/pallas_call | solution.py:756
  (1 shorter events, 0.0 us)
Async XLA Ops:
  0.6 0.7 copy-start
  0.6 0.7 copy-start.1
